TPU v7x, 512 devices: a whole 4x4x16 slice. The times are simulated.
512 devices in a mesh: obs: 16 (over x, y), tm: 32 (over z, core).
Axes of the slice: x: 4, y: 4, z: 16, core: 2. Of those that a mesh axis runs over, the one named last changes fastest.
Arguments:
- flow: float32 [5, 2048, 8192], P(None, 'tm', 'obs'), may hold values from -6 to 6
- point_pos: float32 [3, 8192], P(None, 'obs'), may hold values from -1 to 1
- area_vec: float32 [3, 8192], P(None, 'obs'), may hold values from -3.1819806 to 3.1819806
- observer_angles: float32 [2, 2048], P(None, 'obs'), may hold values from -3.140625 to 3.140625
- band_offset: int32 [16, 16], replicated, may hold values from 0 to 61, as said below
Outputs:
- pressure: float32 [2048, 2048], P('tm', 'obs')
Inputs may be any that keep to these rules, and one draw needn't show every extreme that they name: band_offset[g, b] is the whole number of time steps added to every delay from point block b to observer group g; both 0 and 61 occur.
All inputs are finite; a program needn't handle non-finite values.
Results may differ from a plain program's by a relative error of at most 0.0041.
Values may be sent and summed in bfloat16 or wider, within the bound.
No kernel may reach another device: no remote copies, remote signals or barrier semaphores. Data moves between devices by JAX's collectives and lax.ppermute only.
A program may use at most 64 MiB of HBM per device.

v0:
```python
import math

import jax
import jax.numpy as jnp
from jax import lax
from jax.sharding import PartitionSpec as P

LAGS = 4


FOUR_PI_INV = 1.0 / (4.0 * math.pi)
NEAR_RANGE = 3.25
SOUND_STEP = 1.17
SPHERE_RADIUS = 5.0


def extended(block, sides, width):
    for axis, dim in sides:
        count = lax.axis_size(axis)
        forward = [(i, i + 1) for i in range(count - 1)]
        backward = [(target, source) for source, target in forward]
        low = lax.ppermute(
            lax.slice_in_dim(block, block.shape[dim] - width, None, axis=dim), axis, forward
        )
        high = lax.ppermute(lax.slice_in_dim(block, 0, width, axis=dim), axis, backward)
        block = jnp.concatenate([low, block, high], axis=dim)
    return block


def from_behind(block, axis, distance):
    devices = range(lax.axis_size(axis))
    route = [((i - distance) % len(devices), i) for i in devices]
    return lax.ppermute(block, axis, route)


def passed_along(block, axis, distance):
    devices = range(lax.axis_size(axis))
    route = [(i - distance, i) for i in devices if i - distance in devices]
    return lax.ppermute(block, axis, route)


def observer_xyz(angles):
    azimuth = angles[0]
    elevation = angles[1]
    return SPHERE_RADIUS * jnp.stack(
        [
            jnp.cos(azimuth) * jnp.cos(elevation),
            jnp.sin(azimuth) * jnp.cos(elevation),
            jnp.sin(elevation),
        ]
    )


def source_terms(rimmed, area_vec):
    density = 1.0 + 0.2 * rimmed[0]
    velocity = 0.4 * rimmed[1:4]
    pressure = rimmed[4]
    normal_flux = jnp.sum(velocity * area_vec[:, None, :], axis=0)
    mass_flux = density * normal_flux
    loading = pressure[None] * area_vec[:, None, :] + density[None] * velocity * normal_flux[None]
    stacked = jnp.concatenate([mass_flux[None], loading], axis=0)
    rate_terms = 0.5 * (stacked[:, 2:] - stacked[:, :-2])
    return jnp.concatenate([rate_terms, loading[:, 1:-1]], axis=0).astype(jnp.bfloat16)


def pair_weights(observers, points, lag_count):
    separation = observers[:, None, :] - points[:, :, None]
    distance = jnp.sqrt(jnp.sum(separation * separation, axis=0))
    inverse = 1.0 / distance
    direction = separation * inverse[None]
    lag_steps = (distance - NEAR_RANGE) / SOUND_STEP
    shifts = jnp.arange(lag_count).astype(distance.dtype)
    tent_weights = jnp.maximum(0.0, 1.0 - jnp.abs(shifts[None, :, None] - lag_steps[:, None, :]))
    coeffs = (
        jnp.concatenate(
            [
                inverse[None],
                direction * (inverse / SOUND_STEP)[None],
                direction * (inverse * inverse)[None],
            ],
            axis=0,
        )
        * FOUR_PI_INV
    )
    return (coeffs[:, :, None, :] * tent_weights[None]).astype(jnp.bfloat16)


def placed(shard_terms, weights, offset, buffer_len):
    product = jnp.einsum("kts,kswo->two", shard_terms, weights, preferred_element_type=jnp.float32)
    lag_count = product.shape[1]
    combined = jnp.pad(product[:, 0], ((0, lag_count - 1), (0, 0)))
    for lag_index in range(1, lag_count):
        combined = combined + jnp.pad(
            product[:, lag_index], ((lag_index, lag_count - 1 - lag_index), (0, 0))
        )
    canvas = jnp.zeros((buffer_len, product.shape[2]), jnp.float32)
    return lax.dynamic_update_slice(canvas, combined, (offset, jnp.zeros((), jnp.int32)))


def local(flow, point_pos, area_vec, observer_angles, band_offset):
    rimmed = extended(flow, (("tm", 1),), 1)
    terms = source_terms(rimmed, area_vec)
    block_steps = terms.shape[1]
    buffer_len = 2 * block_steps
    group_size = observer_angles.shape[1]
    own_block = lax.axis_index("obs")
    group_places = observer_xyz(observer_angles)
    delays = lax.dynamic_index_in_dim(band_offset, own_block, 0, keepdims=False)
    every_point = lax.all_gather(point_pos, "obs", axis=1, tiled=True)
    block_points = point_pos.shape[1]
    block_total = lax.axis_size("obs")

    def add_block(accumulated, held_terms, turn_index):
        block_index = (own_block - turn_index) % block_total
        shard_points = lax.dynamic_slice_in_dim(
            every_point, block_index * block_points, block_points, 1
        )
        weights = pair_weights(group_places, shard_points, LAGS)
        return accumulated + placed(held_terms, weights, delays[block_index], buffer_len)

    def turn(state, turn_index):
        accumulated, held_terms = state
        accumulated = add_block(accumulated, held_terms, turn_index)
        held_terms = from_behind(held_terms, "obs", 1)
        return ((accumulated, held_terms), None)

    initial = jnp.zeros((buffer_len, group_size), jnp.float32)
    (accumulated, held_terms), unused = lax.scan(
        turn, (initial, terms), jnp.arange(block_total - 1, dtype=jnp.int32)
    )
    summed = add_block(accumulated, held_terms, jnp.int32(block_total - 1))
    carried = passed_along(summed[block_steps:], "tm", 1)
    return summed[:block_steps] + carried


def solution(mesh):
    in_specs = (P(None, "tm", "obs"), P(None, "obs"), P(None, "obs"), P(None, "obs"), P())
    out_specs = P("tm", "obs")
    return jax.shard_map(local, mesh=mesh, in_specs=in_specs, out_specs=out_specs, check_vma=False)
```

profile of v0, /device:TPU:224, one launch (start us, length us, event | category | flops | bytes accessed | tf_op | source)
XLA Modules:
  0.0 277.9 jit_solution(10183256119806191057)
XLA Ops:
  0.9 1.9 collective-permute-start.2
  2.9 2.4 collective-permute-start.1
  6.8 24.0 %all_gather.3 = f32[3,8192]{1,0:T(4,128)S(1)} all-gather(f32[3,512]{1,0:T(4,128)} %param.8), channel_id=1, replica_groups=mesh['obs'=16,'tm'=32] {'obs'}, dimensions={1}, use_global_device_ids=true | all-gather | bytes 104448 | tf_op jit(solution)/shard_map/all_gather | solution.py:109
  37.4 232.3 %while.18 = (s32[]{:T(128)}, f32[128,128]{1,0:T(8,128)S(1)}, bf16[7,64,512]{2,1,0:T(8,128)(2,1)S(1)}, s32[15]{0:T(128)S(1)}, s32[]{:T(128)}, /*index=5*/s32[16]{...) while((s32[]{:T(128)}, f32[128,128]{1,0:T(8,128)S(1)}, ...), condition=%wide.region_3.4_spmd, body=%wide.region_1.3_spmd.sunk | while | flops 242583056 | bytes 15959524 | solution.py:128
  37.4 3.2 %collective-permute-start = (bf16[7,64,512]{2,1,0:T(8,128)(2,1)S(1)}, bf16[7,64,512]{2,1,0:T(8,128)(2,1)S(1)}, u32[]{:S(2)}, u32[]{:S(2)}) collective-permute-start(bf16[7,64,512]{2,1,0:T(8,128)(2,1)S(1)} %copy.14), channel_id=1, source_target_pairs={{480,0},{0,32},{32,64},{64,96},{96,128},{128,160},{160,192},{192,2... | collective-permute-start | bytes 1376264 | tf_op jit(solution)/shard_map/while/body/eval_jaxpr/ppermute | solution.py:33
  46.5 6.3 %collective-permute-done = bf16[7,64,512]{2,1,0:T(8,128)(2,1)S(1)} collective-permute-done((bf16[7,64,512]{2,1,0:T(8,128)(2,1)S(1)}, bf16[7,64,512]{2,1,0:T(8,128)(2,1)S(1)}, u32[]{:S(2)}, u32[]{:S(2)}) %collective-permute-start) | collective-permute-done | bytes 458784 | tf_op jit(solution)/shard_map/while/body/eval_jaxpr/ppermute | solution.py:33
  52.9 1.9 collective-permute-start
  60.7 6.7 %collective-permute-done = bf16[7,64,512]{2,1,0:T(8,128)(2,1)S(1)} collective-permute-done((bf16[7,64,512]{2,1,0:T(8,128)(2,1)S(1)}, bf16[7,64,512]{2,1,0:T(8,128)(2,1)S(1)}, u32[]{:S(2)}, u32[]{:S(2)}) %collective-permute-start) | collective-permute-done | bytes 458784 | tf_op jit(solution)/shard_map/while/body/eval_jaxpr/ppermute | solution.py:33
  67.4 1.9 collective-permute-start
  75.3 5.8 %collective-permute-done = bf16[7,64,512]{2,1,0:T(8,128)(2,1)S(1)} collective-permute-done((bf16[7,64,512]{2,1,0:T(8,128)(2,1)S(1)}, bf16[7,64,512]{2,1,0:T(8,128)(2,1)S(1)}, u32[]{:S(2)}, u32[]{:S(2)}) %collective-permute-start) | collective-permute-done | bytes 458784 | tf_op jit(solution)/shard_map/while/body/eval_jaxpr/ppermute | solution.py:33
  81.2 1.9 collective-permute-start
  89.1 5.8 %collective-permute-done = bf16[7,64,512]{2,1,0:T(8,128)(2,1)S(1)} collective-permute-done((bf16[7,64,512]{2,1,0:T(8,128)(2,1)S(1)}, bf16[7,64,512]{2,1,0:T(8,128)(2,1)S(1)}, u32[]{:S(2)}, u32[]{:S(2)}) %collective-permute-start) | collective-permute-done | bytes 458784 | tf_op jit(solution)/shard_map/while/body/eval_jaxpr/ppermute | solution.py:33
  94.9 1.9 collective-permute-start
  102.8 5.8 %collective-permute-done = bf16[7,64,512]{2,1,0:T(8,128)(2,1)S(1)} collective-permute-done((bf16[7,64,512]{2,1,0:T(8,128)(2,1)S(1)}, bf16[7,64,512]{2,1,0:T(8,128)(2,1)S(1)}, u32[]{:S(2)}, u32[]{:S(2)}) %collective-permute-start) | collective-permute-done | bytes 458784 | tf_op jit(solution)/shard_map/while/body/eval_jaxpr/ppermute | solution.py:33
  108.6 1.9 collective-permute-start
  116.5 6.5 %collective-permute-done = bf16[7,64,512]{2,1,0:T(8,128)(2,1)S(1)} collective-permute-done((bf16[7,64,512]{2,1,0:T(8,128)(2,1)S(1)}, bf16[7,64,512]{2,1,0:T(8,128)(2,1)S(1)}, u32[]{:S(2)}, u32[]{:S(2)}) %collective-permute-start) | collective-permute-done | bytes 458784 | tf_op jit(solution)/shard_map/while/body/eval_jaxpr/ppermute | solution.py:33
  123.1 1.9 collective-permute-start
  131.0 7.7 %collective-permute-done = bf16[7,64,512]{2,1,0:T(8,128)(2,1)S(1)} collective-permute-done((bf16[7,64,512]{2,1,0:T(8,128)(2,1)S(1)}, bf16[7,64,512]{2,1,0:T(8,128)(2,1)S(1)}, u32[]{:S(2)}, u32[]{:S(2)}) %collective-permute-start) | collective-permute-done | bytes 458784 | tf_op jit(solution)/shard_map/while/body/eval_jaxpr/ppermute | solution.py:33
  138.7 1.9 collective-permute-start
  146.6 8.8 %collective-permute-done = bf16[7,64,512]{2,1,0:T(8,128)(2,1)S(1)} collective-permute-done((bf16[7,64,512]{2,1,0:T(8,128)(2,1)S(1)}, bf16[7,64,512]{2,1,0:T(8,128)(2,1)S(1)}, u32[]{:S(2)}, u32[]{:S(2)}) %collective-permute-start) | collective-permute-done | bytes 458784 | tf_op jit(solution)/shard_map/while/body/eval_jaxpr/ppermute | solution.py:33
  155.4 1.9 collective-permute-start
  163.3 9.9 %collective-permute-done = bf16[7,64,512]{2,1,0:T(8,128)(2,1)S(1)} collective-permute-done((bf16[7,64,512]{2,1,0:T(8,128)(2,1)S(1)}, bf16[7,64,512]{2,1,0:T(8,128)(2,1)S(1)}, u32[]{:S(2)}, u32[]{:S(2)}) %collective-permute-start) | collective-permute-done | bytes 458784 | tf_op jit(solution)/shard_map/while/body/eval_jaxpr/ppermute | solution.py:33
  181.2 10.3 %collective-permute-done = bf16[7,64,512]{2,1,0:T(8,128)(2,1)S(1)} collective-permute-done((bf16[7,64,512]{2,1,0:T(8,128)(2,1)S(1)}, bf16[7,64,512]{2,1,0:T(8,128)(2,1)S(1)}, u32[]{:S(2)}, u32[]{:S(2)}) %collective-permute-start) | collective-permute-done | bytes 458784 | tf_op jit(solution)/shard_map/while/body/eval_jaxpr/ppermute | solution.py:33
  199.5 9.4 %collective-permute-done = bf16[7,64,512]{2,1,0:T(8,128)(2,1)S(1)} collective-permute-done((bf16[7,64,512]{2,1,0:T(8,128)(2,1)S(1)}, bf16[7,64,512]{2,1,0:T(8,128)(2,1)S(1)}, u32[]{:S(2)}, u32[]{:S(2)}) %collective-permute-start) | collective-permute-done | bytes 458784 | tf_op jit(solution)/shard_map/while/body/eval_jaxpr/ppermute | solution.py:33
  216.9 8.6 %collective-permute-done = bf16[7,64,512]{2,1,0:T(8,128)(2,1)S(1)} collective-permute-done((bf16[7,64,512]{2,1,0:T(8,128)(2,1)S(1)}, bf16[7,64,512]{2,1,0:T(8,128)(2,1)S(1)}, u32[]{:S(2)}, u32[]{:S(2)}) %collective-permute-start) | collective-permute-done | bytes 458784 | tf_op jit(solution)/shard_map/while/body/eval_jaxpr/ppermute | solution.py:33
  233.3 7.8 %collective-permute-done = bf16[7,64,512]{2,1,0:T(8,128)(2,1)S(1)} collective-permute-done((bf16[7,64,512]{2,1,0:T(8,128)(2,1)S(1)}, bf16[7,64,512]{2,1,0:T(8,128)(2,1)S(1)}, u32[]{:S(2)}, u32[]{:S(2)}) %collective-permute-start) | collective-permute-done | bytes 458784 | tf_op jit(solution)/shard_map/while/body/eval_jaxpr/ppermute | solution.py:33
  241.2 1.9 collective-permute-start
  249.0 7.0 %collective-permute-done = bf16[7,64,512]{2,1,0:T(8,128)(2,1)S(1)} collective-permute-done((bf16[7,64,512]{2,1,0:T(8,128)(2,1)S(1)}, bf16[7,64,512]{2,1,0:T(8,128)(2,1)S(1)}, u32[]{:S(2)}, u32[]{:S(2)}) %collective-permute-start) | collective-permute-done | bytes 458784 | tf_op jit(solution)/shard_map/while/body/eval_jaxpr/ppermute | solution.py:33
  263.9 5.9 %collective-permute-done = bf16[7,64,512]{2,1,0:T(8,128)(2,1)S(1)} collective-permute-done((bf16[7,64,512]{2,1,0:T(8,128)(2,1)S(1)}, bf16[7,64,512]{2,1,0:T(8,128)(2,1)S(1)}, u32[]{:S(2)}, u32[]{:S(2)}) %collective-permute-start) | collective-permute-done | bytes 458784 | tf_op jit(solution)/shard_map/while/body/eval_jaxpr/ppermute | solution.py:33
  269.7 2.0 fusion.11
  272.1 1.9 collective-permute-start.3
  274.0 3.3 %collective-permute-done.3 = f32[64,128]{1,0:T(8,128)S(1)} collective-permute-done((f32[64,128]{1,0:T(8,128)S(1)}, f32[64,128]{1,0:T(8,128)S(1)}, u32[]{:S(2)}, u32[]{:S(2)}) %collective-permute-start.3) | collective-permute-done | bytes 32800 | tf_op jit(solution)/shard_map/ppermute | solution.py:39
  (249 shorter events, 68.2 us)
Async XLA Ops:
  0.9 35.8 %collective-permute-start.2 = (f32[5,1,512]{2,1,0:T(1,128)S(1)}, f32[5,1,512]{2,1,0:T(1,128)S(1)}, u32[]{:S(2)}, u32[]{:S(2)}) collective-permute-start(f32[5,1,512]{2,1,0:T(1,128)S(1)} %get-tuple-element.143), channel_id=1, source_target_pairs={{1,0},{2,1},{3,2},{4,3},{5,4},{6,5},{7,6},{8,7},{9,8},{10,9},{11,1... | collective-permute-start | bytes 30728 | tf_op jit(solution)/shard_map/ppermute | solution.py:25
  2.9 33.9 %collective-permute-start.1 = (f32[5,1,512]{2,1,0:T(1,128)S(1)}, f32[5,1,512]{2,1,0:T(1,128)S(1)}, u32[]{:S(2)}, u32[]{:S(2)}) collective-permute-start(f32[5,1,512]{2,1,0:T(1,128)S(1)} %get-tuple-element.142), channel_id=1, source_target_pairs={{0,1},{1,2},{2,3},{3,4},{4,5},{5,6},{6,7},{7,8},{8,9},{9,10},{10,1... | collective-permute-start | bytes 30728 | tf_op jit(solution)/shard_map/ppermute | solution.py:22
  32.7 4.1 %copy-start = (f32[5,64,512]{2,1,0:T(8,128)S(1)}, f32[5,64,512]{2,1,0:T(8,128)}, u32[]{:S(2)}) copy-start(f32[5,64,512]{2,1,0:T(8,128)} %param.7) | copy-start | bytes 1966084
  32.9 4.1 %copy-start.1 = (f32[3,512]{1,0:T(4,128)S(1)}, f32[3,512]{1,0:T(4,128)}, u32[]{:S(2)}) copy-start(f32[3,512]{1,0:T(4,128)} %param.9) | copy-start | bytes 18436
  37.4 15.4 %collective-permute-start = (bf16[7,64,512]{2,1,0:T(8,128)(2,1)S(1)}, bf16[7,64,512]{2,1,0:T(8,128)(2,1)S(1)}, u32[]{:S(2)}, u32[]{:S(2)}) collective-permute-start(bf16[7,64,512]{2,1,0:T(8,128)(2,1)S(1)} %copy.14), channel_id=1, source_target_pairs={{480,0},{0,32},{32,64},{64,96},{96,128},{128,160},{160,192},{192,2... | collective-permute-start | bytes 1376264 | tf_op jit(solution)/shard_map/while/body/eval_jaxpr/ppermute | solution.py:33
  52.9 14.5 %collective-permute-start = (bf16[7,64,512]{2,1,0:T(8,128)(2,1)S(1)}, bf16[7,64,512]{2,1,0:T(8,128)(2,1)S(1)}, u32[]{:S(2)}, u32[]{:S(2)}) collective-permute-start(bf16[7,64,512]{2,1,0:T(8,128)(2,1)S(1)} %copy.14), channel_id=1, source_target_pairs={{480,0},{0,32},{32,64},{64,96},{96,128},{128,160},{160,192},{192,2... | collective-permute-start | bytes 1376264 | tf_op jit(solution)/shard_map/while/body/eval_jaxpr/ppermute | solution.py:33
  67.4 13.7 %collective-permute-start = (bf16[7,64,512]{2,1,0:T(8,128)(2,1)S(1)}, bf16[7,64,512]{2,1,0:T(8,128)(2,1)S(1)}, u32[]{:S(2)}, u32[]{:S(2)}) collective-permute-start(bf16[7,64,512]{2,1,0:T(8,128)(2,1)S(1)} %copy.14), channel_id=1, source_target_pairs={{480,0},{0,32},{32,64},{64,96},{96,128},{128,160},{160,192},{192,2... | collective-permute-start | bytes 1376264 | tf_op jit(solution)/shard_map/while/body/eval_jaxpr/ppermute | solution.py:33
  81.2 13.7 %collective-permute-start = (bf16[7,64,512]{2,1,0:T(8,128)(2,1)S(1)}, bf16[7,64,512]{2,1,0:T(8,128)(2,1)S(1)}, u32[]{:S(2)}, u32[]{:S(2)}) collective-permute-start(bf16[7,64,512]{2,1,0:T(8,128)(2,1)S(1)} %copy.14), channel_id=1, source_target_pairs={{480,0},{0,32},{32,64},{64,96},{96,128},{128,160},{160,192},{192,2... | collective-permute-start | bytes 1376264 | tf_op jit(solution)/shard_map/while/body/eval_jaxpr/ppermute | solution.py:33
  94.9 13.7 %collective-permute-start = (bf16[7,64,512]{2,1,0:T(8,128)(2,1)S(1)}, bf16[7,64,512]{2,1,0:T(8,128)(2,1)S(1)}, u32[]{:S(2)}, u32[]{:S(2)}) collective-permute-start(bf16[7,64,512]{2,1,0:T(8,128)(2,1)S(1)} %copy.14), channel_id=1, source_target_pairs={{480,0},{0,32},{32,64},{64,96},{96,128},{128,160},{160,192},{192,2... | collective-permute-start | bytes 1376264 | tf_op jit(solution)/shard_map/while/body/eval_jaxpr/ppermute | solution.py:33
  108.6 14.4 %collective-permute-start = (bf16[7,64,512]{2,1,0:T(8,128)(2,1)S(1)}, bf16[7,64,512]{2,1,0:T(8,128)(2,1)S(1)}, u32[]{:S(2)}, u32[]{:S(2)}) collective-permute-start(bf16[7,64,512]{2,1,0:T(8,128)(2,1)S(1)} %copy.14), channel_id=1, source_target_pairs={{480,0},{0,32},{32,64},{64,96},{96,128},{128,160},{160,192},{192,2... | collective-permute-start | bytes 1376264 | tf_op jit(solution)/shard_map/while/body/eval_jaxpr/ppermute | solution.py:33
  123.1 15.6 %collective-permute-start = (bf16[7,64,512]{2,1,0:T(8,128)(2,1)S(1)}, bf16[7,64,512]{2,1,0:T(8,128)(2,1)S(1)}, u32[]{:S(2)}, u32[]{:S(2)}) collective-permute-start(bf16[7,64,512]{2,1,0:T(8,128)(2,1)S(1)} %copy.14), channel_id=1, source_target_pairs={{480,0},{0,32},{32,64},{64,96},{96,128},{128,160},{160,192},{192,2... | collective-permute-start | bytes 1376264 | tf_op jit(solution)/shard_map/while/body/eval_jaxpr/ppermute | solution.py:33
  138.7 16.7 %collective-permute-start = (bf16[7,64,512]{2,1,0:T(8,128)(2,1)S(1)}, bf16[7,64,512]{2,1,0:T(8,128)(2,1)S(1)}, u32[]{:S(2)}, u32[]{:S(2)}) collective-permute-start(bf16[7,64,512]{2,1,0:T(8,128)(2,1)S(1)} %copy.14), channel_id=1, source_target_pairs={{480,0},{0,32},{32,64},{64,96},{96,128},{128,160},{160,192},{192,2... | collective-permute-start | bytes 1376264 | tf_op jit(solution)/shard_map/while/body/eval_jaxpr/ppermute | solution.py:33
  155.4 17.8 %collective-permute-start = (bf16[7,64,512]{2,1,0:T(8,128)(2,1)S(1)}, bf16[7,64,512]{2,1,0:T(8,128)(2,1)S(1)}, u32[]{:S(2)}, u32[]{:S(2)}) collective-permute-start(bf16[7,64,512]{2,1,0:T(8,128)(2,1)S(1)} %copy.14), channel_id=1, source_target_pairs={{480,0},{0,32},{32,64},{64,96},{96,128},{128,160},{160,192},{192,2... | collective-permute-start | bytes 1376264 | tf_op jit(solution)/shard_map/while/body/eval_jaxpr/ppermute | solution.py:33
  173.3 18.2 %collective-permute-start = (bf16[7,64,512]{2,1,0:T(8,128)(2,1)S(1)}, bf16[7,64,512]{2,1,0:T(8,128)(2,1)S(1)}, u32[]{:S(2)}, u32[]{:S(2)}) collective-permute-start(bf16[7,64,512]{2,1,0:T(8,128)(2,1)S(1)} %copy.14), channel_id=1, source_target_pairs={{480,0},{0,32},{32,64},{64,96},{96,128},{128,160},{160,192},{192,2... | collective-permute-start | bytes 1376264 | tf_op jit(solution)/shard_map/while/body/eval_jaxpr/ppermute | solution.py:33
  191.5 17.4 %collective-permute-start = (bf16[7,64,512]{2,1,0:T(8,128)(2,1)S(1)}, bf16[7,64,512]{2,1,0:T(8,128)(2,1)S(1)}, u32[]{:S(2)}, u32[]{:S(2)}) collective-permute-start(bf16[7,64,512]{2,1,0:T(8,128)(2,1)S(1)} %copy.14), channel_id=1, source_target_pairs={{480,0},{0,32},{32,64},{64,96},{96,128},{128,160},{160,192},{192,2... | collective-permute-start | bytes 1376264 | tf_op jit(solution)/shard_map/while/body/eval_jaxpr/ppermute | solution.py:33
  208.9 16.5 %collective-permute-start = (bf16[7,64,512]{2,1,0:T(8,128)(2,1)S(1)}, bf16[7,64,512]{2,1,0:T(8,128)(2,1)S(1)}, u32[]{:S(2)}, u32[]{:S(2)}) collective-permute-start(bf16[7,64,512]{2,1,0:T(8,128)(2,1)S(1)} %copy.14), channel_id=1, source_target_pairs={{480,0},{0,32},{32,64},{64,96},{96,128},{128,160},{160,192},{192,2... | collective-permute-start | bytes 1376264 | tf_op jit(solution)/shard_map/while/body/eval_jaxpr/ppermute | solution.py:33
  225.5 15.7 %collective-permute-start = (bf16[7,64,512]{2,1,0:T(8,128)(2,1)S(1)}, bf16[7,64,512]{2,1,0:T(8,128)(2,1)S(1)}, u32[]{:S(2)}, u32[]{:S(2)}) collective-permute-start(bf16[7,64,512]{2,1,0:T(8,128)(2,1)S(1)} %copy.14), channel_id=1, source_target_pairs={{480,0},{0,32},{32,64},{64,96},{96,128},{128,160},{160,192},{192,2... | collective-permute-start | bytes 1376264 | tf_op jit(solution)/shard_map/while/body/eval_jaxpr/ppermute | solution.py:33
  241.2 14.8 %collective-permute-start = (bf16[7,64,512]{2,1,0:T(8,128)(2,1)S(1)}, bf16[7,64,512]{2,1,0:T(8,128)(2,1)S(1)}, u32[]{:S(2)}, u32[]{:S(2)}) collective-permute-start(bf16[7,64,512]{2,1,0:T(8,128)(2,1)S(1)} %copy.14), channel_id=1, source_target_pairs={{480,0},{0,32},{32,64},{64,96},{96,128},{128,160},{160,192},{192,2... | collective-permute-start | bytes 1376264 | tf_op jit(solution)/shard_map/while/body/eval_jaxpr/ppermute | solution.py:33
  256.0 13.7 %collective-permute-start = (bf16[7,64,512]{2,1,0:T(8,128)(2,1)S(1)}, bf16[7,64,512]{2,1,0:T(8,128)(2,1)S(1)}, u32[]{:S(2)}, u32[]{:S(2)}) collective-permute-start(bf16[7,64,512]{2,1,0:T(8,128)(2,1)S(1)} %copy.14), channel_id=1, source_target_pairs={{480,0},{0,32},{32,64},{64,96},{96,128},{128,160},{160,192},{192,2... | collective-permute-start | bytes 1376264 | tf_op jit(solution)/shard_map/while/body/eval_jaxpr/ppermute | solution.py:33
  272.1 5.2 %collective-permute-start.3 = (f32[64,128]{1,0:T(8,128)S(1)}, f32[64,128]{1,0:T(8,128)S(1)}, u32[]{:S(2)}, u32[]{:S(2)}) collective-permute-start(f32[64,128]{1,0:T(8,128)S(1)} %slice.102), channel_id=1, source_target_pairs={{0,1},{1,2},{2,3},{3,4},{4,5},{5,6},{6,7},{7,8},{8,9},{9,10},{10,1... | collective-permute-start | bytes 98312 | tf_op jit(solution)/shard_map/ppermute | solution.py:39
where the time goes:
time: 280 us; the launch traced here: 278 us
  waiting for transfers between devices  116 us (41%)
  loops' own time  39.4 us (14%)
  starting transfers between devices  36.3 us (13%)
  local copies, waits for them, and re-layouts  27.2 us (10%)
  blocking collectives  24 us (9%)
  other arithmetic  20.2 us (7%)
  matrix products  13.2 us (5%)
    ppermute x15, waiting for transfers between devices, from_behind(): return lax.ppermute(block, axis, route)  112 us
    another operation x1, loops' own time, local(): lax.scan(turn, (initial, terms), jnp.arange(block_total - 1, dtype=jnp.in...  39.4 us
    ppermute x15, starting transfers between devices, from_behind(): return lax.ppermute(block, axis, route)  30.1 us
    all_gather x1, blocking collectives, local(): every_point = lax.all_gather(point_pos, 'obs', axis=1, tiled=True)  24 us
    dot_general x16, matrix products, placed(): jnp.einsum('kts,kswo->two', shard_terms, weights, preferred_element_type=...  13.2 us
    dynamic_slice x16, local copies, waits for them, and re-layouts, add_block(): delays[block_index]  10.3 us
    dynamic_slice x15, local copies, waits for them, and re-layouts, local(): lax.scan(turn, (initial, terms), jnp.arange(block_total - 1, dtype=jnp.in...  9.08 us
  transfers between devices with their start and end apart: 18, of which 16 were waited for; matrix products, arithmetic and copies ran while one was open for 20% of the time, Pallas kernels for 0%

commit v1 on v0

v1 whole, which is shorter than its diff:
```python
import math

import jax
import jax.numpy as jnp
from jax import lax
from jax.experimental import pallas as pl
from jax.experimental.pallas import tpu as pltpu
from jax.sharding import PartitionSpec as P

LAGS = 4
FOUR_PI_INV = 1.0 / (4.0 * math.pi)
NEAR_RANGE = 3.25
SOUND_STEP = 1.17
SPHERE_RADIUS = 5.0
COMPS = 4
BACK = 8
CHUNK = 16


def terms_kernel(edge_ref, flow_ref, low_ref, high_ref, area_ref, point_ref, terms_ref, spread_ref, rows_ref):
    steps = flow_ref.shape[1]
    rows_ref[:, :BACK, :] = jnp.zeros_like(rows_ref[:, :BACK, :])
    rows_ref[:, BACK + steps :, :] = jnp.zeros_like(rows_ref[:, BACK + steps :, :])
    rows_ref[:, BACK - LAGS : BACK, :] = low_ref[...]
    rows_ref[:, BACK : BACK + steps, :] = flow_ref[...]
    rows_ref[:, BACK + steps : BACK + steps + 1, :] = high_ref[...]
    area = [area_ref[i : i + 1, :] for i in range(3)]
    point = [point_ref[i : i + 1, :] for i in range(3)]
    density = 1.0 + 0.2 * rows_ref[0]
    velocity = [0.4 * rows_ref[1 + i] for i in range(3)]
    pressure = rows_ref[4]
    normal_flux = velocity[0] * area[0] + velocity[1] * area[1] + velocity[2] * area[2]
    mass_flux = density * normal_flux
    loading = [pressure * area[i] + mass_flux * velocity[i] for i in range(3)]
    reach = SPHERE_RADIUS**2 + point[0] * point[0] + point[1] * point[1] + point[2] * point[2]
    first = BACK - LAGS + 1
    count = steps + LAGS - 1
    row = lax.broadcasted_iota(jnp.int32, (count, area_ref.shape[1]), 0)
    keep = jnp.logical_or(row >= LAGS - 1, edge_ref[0] != 0)

    def rate(x):
        return 0.5 * (x[first + 1 : first + 1 + count] - x[first - 1 : first - 1 + count])

    mass_rate = rate(mass_flux)
    load_rate = [rate(x) for x in loading]
    load = [x[first : first + count] for x in loading]
    along_rate = point[0] * load_rate[0] + point[1] * load_rate[1] + point[2] * load_rate[2]
    along = point[0] * load[0] + point[1] * load[1] + point[2] * load[2]
    far = load_rate + [-along_rate]
    near = [load[i] - (2.0 * point[i]) * mass_rate for i in range(3)] + [reach * mass_rate - along]
    width = area_ref.shape[1]
    for family, parts in enumerate((far, near)):
        for comp, part in enumerate(parts):
            part = jnp.where(keep, part, 0.0)
            for lag in range(LAGS):
                start = LAGS - 1 - lag
                terms_ref[comp * steps : (comp + 1) * steps, pl.ds((family * LAGS + lag) * width, width)] = part[
                    start : start + steps
                ].astype(jnp.bfloat16)
    turned = jnp.transpose(jnp.concatenate([point_ref[...], jnp.zeros((5, width), jnp.float32)], axis=0))
    for i in range(3):
        spread_ref[i] = jnp.broadcast_to(turned[:, i : i + 1], spread_ref.shape[1:])


def fill_weights(places, spread_ref, weights_ref):
    width = spread_ref.shape[1]
    lanes = places[0].shape[1] // spread_ref.shape[2]
    for start in range(0, width, CHUNK):
        sep = [
            places[i] - jnp.concatenate([spread_ref[i, start : start + CHUNK, :]] * lanes, axis=1) for i in range(3)
        ]
        square = sep[0] * sep[0] + sep[1] * sep[1] + sep[2] * sep[2]
        inverse = lax.rsqrt(square)
        lag = (square * inverse) * (1.0 / SOUND_STEP) - (NEAR_RANGE / SOUND_STEP)
        behind = 1.0 - lag
        beyond = lag - 2.0
        tents = (
            jnp.maximum(behind, 0.0),
            jnp.maximum(jnp.minimum(lag, 2.0 - lag), 0.0),
            jnp.maximum(jnp.minimum(lag - 1.0, 3.0 - lag), 0.0),
            jnp.maximum(beyond, 0.0),
        )
        inverse_square = inverse * inverse
        far = inverse_square * (FOUR_PI_INV / SOUND_STEP)
        near = (inverse_square * inverse) * FOUR_PI_INV
        for family, coeff in enumerate((far, near)):
            for index, tent in enumerate(tents):
                base = (family * LAGS + index) * width + start
                weights_ref[base : base + CHUNK, :] = (coeff * tent).astype(jnp.bfloat16)


def pair_kernel(angle_ref, terms_ref, spread_ref, sums_ref, places_ref, weights_ref):
    step = pl.program_id(0)

    @pl.when(step == 0)
    def _():
        azimuth = angle_ref[:, 0, :]
        elevation = angle_ref[:, 1, :]
        flat = SPHERE_RADIUS * jnp.cos(elevation)
        places_ref[0] = flat * jnp.cos(azimuth)
        places_ref[1] = flat * jnp.sin(azimuth)
        places_ref[2] = SPHERE_RADIUS * jnp.sin(elevation)

    pair = sums_ref.shape[0]
    places = [
        jnp.concatenate([places_ref[i, pl.ds(step * pair + j, 1), :] for j in range(pair)], axis=1) for i in range(3)
    ]
    fill_weights(places, spread_ref, weights_ref)
    product = jnp.dot(terms_ref[...], weights_ref[...], preferred_element_type=jnp.float32)
    steps = sums_ref.shape[1]
    lanes = sums_ref.shape[2]
    total = product[3 * steps :]
    for i in range(3):
        total = total + places[i] * product[i * steps : (i + 1) * steps]
    for j in range(pair):
        sums_ref[j] = total[:, j * lanes : (j + 1) * lanes]


def place_kernel(offset_ref, sums_ref, out_ref, later_ref, canvas_ref):
    groups, steps, lanes = sums_ref.shape
    canvas_ref[...] = jnp.zeros_like(canvas_ref)
    for block in range(groups):
        span = pl.ds(offset_ref[block], steps)
        canvas_ref[span, :] = canvas_ref[span, :] + sums_ref[block]
    out_ref[...] = canvas_ref[:steps]
    later_ref[...] = canvas_ref[steps : 2 * steps]


VMEM = pl.BlockSpec(memory_space=pltpu.VMEM)
SMEM = pl.BlockSpec(memory_space=pltpu.SMEM)


def local(flow, point_pos, area_vec, observer_angles, band_offset):
    steps = flow.shape[1]
    width = flow.shape[2]
    groups = lax.axis_size("obs")
    lanes = observer_angles.shape[1]
    times = lax.axis_size("tm")
    angles = lax.all_to_all(
        jnp.broadcast_to(observer_angles[None], (groups, 2, lanes)), "obs", 0, 0, tiled=True
    )
    low = lax.ppermute(flow[:, steps - LAGS :], "tm", [(i, i + 1) for i in range(times - 1)])
    high = lax.ppermute(flow[:, :1], "tm", [(i + 1, i) for i in range(times - 1)])
    edge = lax.axis_index("tm").astype(jnp.int32).reshape(1)
    depth = 2 * LAGS * width
    terms, spread = pl.pallas_call(
        terms_kernel,
        out_shape=(
            jax.ShapeDtypeStruct((COMPS * steps, depth), jnp.bfloat16),
            jax.ShapeDtypeStruct((3, width, lanes), jnp.float32),
        ),
        in_specs=[SMEM] + [VMEM] * 5,
        out_specs=(VMEM, VMEM),
        scratch_shapes=[pltpu.VMEM((5, steps + 2 * BACK, width), jnp.float32)],
        name="terms",
    )(edge, flow, low, high, area_vec, point_pos)
    pair = 2
    sums = pl.pallas_call(
        pair_kernel,
        grid=(groups // pair,),
        out_shape=jax.ShapeDtypeStruct((groups, steps, lanes), jnp.float32),
        in_specs=[VMEM] * 3,
        out_specs=pl.BlockSpec((pair, steps, lanes), lambda i: (i, 0, 0)),
        scratch_shapes=[
            pltpu.VMEM((3, groups, lanes), jnp.float32),
            pltpu.VMEM((depth, pair * lanes), jnp.bfloat16),
        ],
        name="pairs",
    )(angles, terms, spread)
    sums = lax.all_to_all(sums, "obs", 0, 0, tiled=True)
    offsets = lax.dynamic_index_in_dim(band_offset, lax.axis_index("obs"), 0, keepdims=False)
    out, later = pl.pallas_call(
        place_kernel,
        out_shape=(jax.ShapeDtypeStruct((steps, lanes), jnp.float32),) * 2,
        in_specs=[SMEM, VMEM],
        out_specs=(VMEM, VMEM),
        scratch_shapes=[pltpu.VMEM((2 * steps, lanes), jnp.float32)],
        name="place",
    )(offsets, sums)
    carried = lax.ppermute(later, "tm", [(i, i + 1) for i in range(times - 1)])
    return out + carried


def solution(mesh):
    in_specs = (P(None, "tm", "obs"), P(None, "obs"), P(None, "obs"), P(None, "obs"), P())
    out_specs = P("tm", "obs")
    return jax.shard_map(local, mesh=mesh, in_specs=in_specs, out_specs=out_specs, check_vma=False)
```

time: 280 us -> 65.6 us (0.23)
  the two profiles are of different devices: /device:TPU:224 before, /device:TPU:128 now
where the time goes in v1:
time: 65.6 us; the launch traced here: 65.1 us
  starting transfers between devices  22.4 us (34%)
  waiting for transfers between devices  17.9 us (27%)
  Pallas kernels  17.6 us (27%)
  local copies, waits for them, and re-layouts  5.7 us (9%)
  other arithmetic  1.38 us (2%)
    pallas_call x1, Pallas kernels, local(): pl.pallas_call(pair_kernel, grid=(groups // pair,), out_shape=jax.ShapeDt...  12.1 us
    all_to_all x1, waiting for transfers between devices, local(): sums = lax.all_to_all(sums, 'obs', 0, 0, tiled=True)  11.8 us
    all_to_all x1, starting transfers between devices, local(): lax.all_to_all(jnp.broadcast_to(observer_angles[None], (groups, 2, lanes)...  7.03 us
    all_to_all x1, starting transfers between devices, local(): sums = lax.all_to_all(sums, 'obs', 0, 0, tiled=True)  6.94 us
    ppermute x1, waiting for transfers between devices, local(): carried = lax.ppermute(later, 'tm', [(i, i + 1) for i in range(times - 1)])  4.73 us
    ppermute x1, starting transfers between devices, local(): lax.ppermute(flow[:, :1], 'tm', [(i + 1, i) for i in range(times - 1)])  4.56 us
    pallas_call x1, Pallas kernels, local(): pl.pallas_call(terms_kernel, out_shape=(jax.ShapeDtypeStruct((COMPS * ste...  3.71 us
    unnamed x10, local copies, waits for them, and re-layouts  2.02 us
  transfers between devices with their start and end apart: 5, of which 3 were waited for; matrix products, arithmetic and copies ran while one was open for 4% of the time, Pallas kernels for 6%

profile of v1, /device:TPU:128, one launch (start us, length us, event | category | flops | bytes accessed | tf_op | source)
XLA Modules:
  0.0 65.1 jit_solution(16467018730734937391)
XLA Ops:
  0.0 0.0 copy-start
  0.0 0.9 %slice.6 = f32[5,4,512]{2,1,0:T(4,128)S(1)} slice(f32[5,64,512]{2,1,0:T(8,128)} %flow_ref.1), slice={[0:5], [60:64], [0:512]} | slice | bytes 81920 | tf_op jit(solution)/shard_map/slice | solution.py:142
  0.9 1.9 %collective-permute-start = (f32[5,4,512]{2,1,0:T(4,128)S(1)}, f32[5,4,512]{2,1,0:T(4,128)S(1)}, u32[]{:S(2)}, u32[]{:S(2)}) collective-permute-start(f32[5,4,512]{2,1,0:T(4,128)S(1)} %slice.6), channel_id=1, source_target_pairs={{0,1},{1,2},{2,3},{3,4},{4,5},{5,6},{6,7},{7,8},{8,9},{9,10},{10,1... | collective-permute-start | bytes 122888 | tf_op jit(solution)/shard_map/ppermute | solution.py:142
  2.8 1.3 %broadcast_in_dim.2 = f32[16,2,128]{2,1,0:T(2,128)} broadcast(f32[2,128]{1,0:T(2,128)} %param.8), dimensions={1,2} | broadcast | bytes 17408 | tf_op jit(solution)/shard_map/broadcast_in_dim | solution.py:140
  4.1 7.0 %all-to-all-start = ((f32[16,2,128]{2,1,0:T(2,128)}), f32[16,2,128]{2,1,0:T(2,128)S(1)}, u32[]{:S(2)}, u32[]{:S(2)}) async-start(f32[16,2,128]{2,1,0:T(2,128)} %broadcast_in_dim.2), calls=%async_computation | async-start | bytes 32768 | tf_op jit(solution)/shard_map/all_to_all | solution.py:139
  11.2 0.9 %slice.7 = f32[5,1,512]{2,1,0:T(1,128)S(1)} slice(f32[5,64,512]{2,1,0:T(8,128)} %flow_ref.1), slice={[0:5], [0:1], [0:512]} | slice | bytes 20480 | tf_op jit(solution)/shard_map/slice | solution.py:143
  12.1 4.6 %collective-permute-start.1 = (f32[5,1,512]{2,1,0:T(1,128)S(1)}, f32[5,1,512]{2,1,0:T(1,128)S(1)}, u32[]{:S(2)}, u32[]{:S(2)}) collective-permute-start(f32[5,1,512]{2,1,0:T(1,128)S(1)} %slice.7), channel_id=1, source_target_pairs={{1,0},{2,1},{3,2},{4,3},{5,4},{6,5},{7,6},{8,7},{9,8},{10,9},{11,1... | collective-permute-start | bytes 30728 | tf_op jit(solution)/shard_map/ppermute | solution.py:143
  16.6 1.4 %collective-permute-done.1.high_ref = f32[5,1,512]{2,1,0:T(1,128)S(1)} collective-permute-done((f32[5,1,512]{2,1,0:T(1,128)S(1)}, f32[5,1,512]{2,1,0:T(1,128)S(1)}, u32[]{:S(2)}, u32[]{:S(2)}) %collective-permute-start.1) | collective-permute-done | bytes 10272 | tf_op jit(solution)/shard_map/ppermute | solution.py:143
  18.0 0.0 copy-start.4
  18.0 0.0 collective-permute-done.low_ref
  18.0 0.0 copy-start.3
  18.0 0.6 copy-done.4
  18.6 0.0 copy-done.3
  18.6 3.7 %terms.1 = (bf16[256,4096]{1,0:T(8,128)(2,1)}, f32[3,512,128]{2,1,0:T(8,128)}) custom-call(s32[1]{0:T(128)} %bitcast.1.edge_ref, f32[5,64,512]{2,1,0:T(8,128)} %flow_ref.1, f32[5,4,512]{2,1,0:T(4,128)} %copy-done.3, f32[5,1,512]{2,1,0:T(1,128)} %copy-done.4, f32[3,512]{1,0:T(4,128)} %area_ref.1, f32[3,512]{1,0:T(4,128)} %point_ref.1), custom_call_target="tpu_custom_call" | custom-call | tf_op jit(solution)/shard_map/terms/pallas_call | solution.py:146
  22.3 0.0 all-to-all-done.angle_ref
  22.3 0.0 copy-start.2
  22.3 0.6 copy-done.2
  22.9 12.1 %pairs.1 = f32[16,64,128]{2,1,0:T(8,128)} custom-call(f32[16,2,128]{2,1,0:T(2,128)} %copy-done.2, bf16[256,4096]{1,0:T(8,128)(2,1)} %get-tuple-element.9.terms_ref, f32[3,512,128]{2,1,0:T(8,128)} %get-tuple-element.10.spread_ref), custom_call_target="tpu_custom_call" | custom-call | tf_op jit(solution)/shard_map/pairs/pallas_call | solution.py:158
  35.1 6.9 %all-to-all-start.1 = ((f32[16,64,128]{2,1,0:T(8,128)}), f32[16,64,128]{2,1,0:T(8,128)S(1)}, u32[]{:S(2)}, u32[]{:S(2)}) async-start(f32[16,64,128]{2,1,0:T(8,128)} %pairs.1), calls=%async_computation.1 | async-start | bytes 1048576 | tf_op jit(solution)/shard_map/all_to_all | solution.py:170
  42.0 0.0 copy-done
  42.0 0.6 dynamic-slice_bitcast_fusion.offset_ref
  42.6 11.8 %all-to-all-done.1.sums_ref = f32[16,64,128]{2,1,0:T(8,128)S(1)} async-done(((f32[16,64,128]{2,1,0:T(8,128)}), f32[16,64,128]{2,1,0:T(8,128)S(1)}, u32[]{:S(2)}, u32[]{:S(2)}) %all-to-all-start.1) | async-done | bytes 524320 | tf_op jit(solution)/shard_map/all_to_all | solution.py:170
  54.5 0.0 copy-start.1
  54.5 0.8 %copy-done.1 = f32[16,64,128]{2,1,0:T(8,128)} copy-done((f32[16,64,128]{2,1,0:T(8,128)}, f32[16,64,128]{2,1,0:T(8,128)S(1)}, u32[]{:S(2)}) %copy-start.1) | copy-done | bytes 524312
  55.3 1.8 %place.1 = (f32[64,128]{1,0:T(8,128)}, f32[64,128]{1,0:T(8,128)}) custom-call(s32[16]{0:T(128)} %dynamic-slice_bitcast_fusion.offset_ref, f32[16,64,128]{2,1,0:T(8,128)} %copy-done.1), custom_call_target="tpu_custom_call" | custom-call | tf_op jit(solution)/shard_map/place/pallas_call | solution.py:172
  57.1 1.9 %collective-permute-start.2 = (f32[64,128]{1,0:T(8,128)}, f32[64,128]{1,0:T(8,128)S(1)}, u32[]{:S(2)}, u32[]{:S(2)}) collective-permute-start(f32[64,128]{1,0:T(8,128)} %get-tuple-element.12), channel_id=1, source_target_pairs={{0,1},{1,2},{2,3},{3,4},{4,5},{5,6},{6,7},{7,8},{8,9},{9,10},{10,1... | collective-permute-start | bytes 98312 | tf_op jit(solution)/shard_map/ppermute | solution.py:180
  59.0 4.7 %collective-permute-done.2 = f32[64,128]{1,0:T(8,128)S(1)} collective-permute-done((f32[64,128]{1,0:T(8,128)}, f32[64,128]{1,0:T(8,128)S(1)}, u32[]{:S(2)}, u32[]{:S(2)}) %collective-permute-start.2) | collective-permute-done | bytes 32800 | tf_op jit(solution)/shard_map/ppermute | solution.py:180
  63.7 1.4 %add.8 = f32[64,128]{1,0:T(8,128)} add(f32[64,128]{1,0:T(8,128)} %get-tuple-element.11, f32[64,128]{1,0:T(8,128)S(1)} %collective-permute-done.2) | non-fusion elementwise | flops 8192 | bytes 98304 | tf_op jit(solution)/shard_map/add | solution.py:181
Async XLA Ops:
  0.0 42.0 %copy-start = (s32[16,16]{1,0:T(8,128)S(1)}, s32[16,16]{1,0:T(8,128)}, u32[]{:S(2)}) copy-start(s32[16,16]{1,0:T(8,128)} %param.9) | copy-start | bytes 3076
  0.9 17.1 %collective-permute-start = (f32[5,4,512]{2,1,0:T(4,128)S(1)}, f32[5,4,512]{2,1,0:T(4,128)S(1)}, u32[]{:S(2)}, u32[]{:S(2)}) collective-permute-start(f32[5,4,512]{2,1,0:T(4,128)S(1)} %slice.6), channel_id=1, source_target_pairs={{0,1},{1,2},{2,3},{3,4},{4,5},{5,6},{6,7},{7,8},{8,9},{9,10},{10,1... | collective-permute-start | bytes 122888 | tf_op jit(solution)/shard_map/ppermute | solution.py:142
  4.1 18.2 %all-to-all-start = ((f32[16,2,128]{2,1,0:T(2,128)}), f32[16,2,128]{2,1,0:T(2,128)S(1)}, u32[]{:S(2)}, u32[]{:S(2)}) async-start(f32[16,2,128]{2,1,0:T(2,128)} %broadcast_in_dim.2), calls=%async_computation | async-start | bytes 32768 | tf_op jit(solution)/shard_map/all_to_all | solution.py:139
  12.1 5.9 %collective-permute-start.1 = (f32[5,1,512]{2,1,0:T(1,128)S(1)}, f32[5,1,512]{2,1,0:T(1,128)S(1)}, u32[]{:S(2)}, u32[]{:S(2)}) collective-permute-start(f32[5,1,512]{2,1,0:T(1,128)S(1)} %slice.7), channel_id=1, source_target_pairs={{1,0},{2,1},{3,2},{4,3},{5,4},{6,5},{7,6},{8,7},{9,8},{10,9},{11,1... | collective-permute-start | bytes 30728 | tf_op jit(solution)/shard_map/ppermute | solution.py:143
  18.0 0.6 copy-start.4
  18.0 0.6 copy-start.3
  22.3 0.6 copy-start.2
  35.1 19.4 %all-to-all-start.1 = ((f32[16,64,128]{2,1,0:T(8,128)}), f32[16,64,128]{2,1,0:T(8,128)S(1)}, u32[]{:S(2)}, u32[]{:S(2)}) async-start(f32[16,64,128]{2,1,0:T(8,128)} %pairs.1), calls=%async_computation.1 | async-start | bytes 1048576 | tf_op jit(solution)/shard_map/all_to_all | solution.py:170
  54.5 0.8 %copy-start.1 = (f32[16,64,128]{2,1,0:T(8,128)}, f32[16,64,128]{2,1,0:T(8,128)S(1)}, u32[]{:S(2)}) copy-start(f32[16,64,128]{2,1,0:T(8,128)S(1)} %all-to-all-done.1.sums_ref) | copy-start | bytes 1572868
  57.1 6.6 %collective-permute-start.2 = (f32[64,128]{1,0:T(8,128)}, f32[64,128]{1,0:T(8,128)S(1)}, u32[]{:S(2)}, u32[]{:S(2)}) collective-permute-start(f32[64,128]{1,0:T(8,128)} %get-tuple-element.12), channel_id=1, source_target_pairs={{0,1},{1,2},{2,3},{3,4},{4,5},{5,6},{6,7},{7,8},{8,9},{9,10},{10,1... | collective-permute-start | bytes 98312 | tf_op jit(solution)/shard_map/ppermute | solution.py:180

commit v2 on v1

v2 whole, which is shorter than its diff:
```python
import math

import jax
import jax.numpy as jnp
from jax import lax
from jax.experimental import pallas as pl
from jax.experimental.pallas import tpu as pltpu
from jax.sharding import PartitionSpec as P

LAGS = 4
NEAR_RANGE = 3.25
SOUND_STEP = 1.17
RADIUS = 5.0 / SOUND_STEP
NEAREST = NEAR_RANGE / SOUND_STEP
SCALE = 1.0 / (4.0 * math.pi * SOUND_STEP * SOUND_STEP)
COMPS = 4
ROWS = 8
LANES = 128
CHUNK = 16
PARTS = 8
LEAD = 0


def prep_kernel(flow_ref, angle_ref, wide_ref, low_ref, high_ref, edges_ref, sem):
    steps = flow_ref.shape[1]
    copies = [
        pltpu.make_async_copy(flow_ref.at[:, pl.ds(start, ROWS), :], edges_ref.at[side], sem.at[side])
        for side, start in enumerate((steps - ROWS, 0))
    ]
    for copy in copies:
        copy.start()
    for group in range(wide_ref.shape[0]):
        wide_ref[group] = angle_ref[...]
    for copy in copies:
        copy.wait()
    low_ref[...] = edges_ref[0, :, ROWS - LAGS :, :]
    high_ref[...] = edges_ref[1, :, :1, :]


def terms_kernel(edge_ref, flow_ref, low_ref, high_ref, area_ref, point_ref, terms_ref, spread_ref, field_ref, part_ref):
    steps = flow_ref.shape[1]
    width = flow_ref.shape[2]
    count = steps + ROWS
    for cut in range(width // LANES):
        lanes = slice(cut * LANES, (cut + 1) * LANES)
        area = [SCALE * area_ref[i : i + 1, lanes] for i in range(3)]
        point = [(1.0 / SOUND_STEP) * point_ref[i : i + 1, lanes] for i in range(3)]

        def fields(source, start, rows):
            density = 1.0 + 0.2 * source[0, :, lanes]
            velocity = [0.4 * source[1 + i, :, lanes] for i in range(3)]
            pressure = source[4, :, lanes]
            normal_flux = velocity[0] * area[0] + velocity[1] * area[1] + velocity[2] * area[2]
            mass_flux = density * normal_flux
            field_ref[0, cut, start : start + rows, :] = mass_flux
            for i in range(3):
                field_ref[1 + i, cut, start : start + rows, :] = pressure * area[i] + mass_flux * velocity[i]

        field_ref[:, cut, ROWS + steps :, :] = jnp.zeros((4, ROWS, LANES), jnp.float32)
        fields(low_ref, ROWS - LAGS, LAGS)
        fields(flow_ref, ROWS, steps)
        fields(high_ref, ROWS + steps, 1)
        first = ROWS - LAGS + 1
        row = lax.broadcasted_iota(jnp.int32, (count, LANES), 0)
        keep = jnp.where(jnp.logical_or(row >= LAGS - 1, edge_ref[0] != 0), 1.0, 0.0)
        rates = [
            (0.5 * keep)
            * (field_ref[k, cut, first + 1 : first + 1 + count, :] - field_ref[k, cut, first - 1 : first - 1 + count, :])
            for k in range(4)
        ]
        loads = [keep * field_ref[1 + i, cut, first : first + count, :] for i in range(3)]
        reach = RADIUS * RADIUS + point[0] * point[0] + point[1] * point[1] + point[2] * point[2]
        mass_rate = SOUND_STEP * rates[0]
        far = rates[1:] + [-(point[0] * rates[1] + point[1] * rates[2] + point[2] * rates[3])]
        near = [loads[i] - (2.0 * point[i]) * mass_rate for i in range(3)]
        near.append(reach * mass_rate - (point[0] * loads[0] + point[1] * loads[1] + point[2] * loads[2]))
        for family, parts in enumerate((far, near)):
            for comp, part in enumerate(parts):
                part_ref[cut, family * COMPS + comp] = part
        for family in range(2):
            for comp in range(COMPS):
                for lag in range(LAGS):
                    start = LAGS - 1 - lag
                    block = (cut * 2 + family) * LAGS + lag
                    terms_ref[block, comp * steps : (comp + 1) * steps, :] = part_ref[
                        cut, family * COMPS + comp, start : start + steps, :
                    ].astype(jnp.bfloat16)
        turned = jnp.transpose(
            jnp.concatenate([2.0 * point[0], 2.0 * point[1], 2.0 * point[2], reach] * 2, axis=0)
        )
        for i in range(4):
            spread_ref[i, lanes, :] = jnp.broadcast_to(turned[:, i : i + 1], (LANES, LANES))


def fill_weights(places, spread_ref, weights_ref, half, part):
    span = spread_ref.shape[1] // 2
    for start in range(span * part // PARTS, span * (part + 1) // PARTS, CHUNK):
        rows = slice(half * span + start, half * span + start + CHUNK)
        spread = [spread_ref[i, rows, :] for i in range(4)]
        for group, place in enumerate(places):
            square = spread[3] - place[0] * spread[0] - place[1] * spread[1] - place[2] * spread[2]
            inverse = lax.rsqrt(square)
            behind = (1.0 + NEAREST) - square * inverse
            first = jnp.maximum(behind, 0.0)
            passed = first - behind
            last = jnp.maximum(passed - 1.0, 0.0)
            middle = jnp.minimum(passed, 1.0)
            tents = (first, (1.0 - middle) - first, middle - last, last)
            far = inverse * inverse
            near = far * inverse
            quarter = start // LANES
            for family, coeff in enumerate((far, near)):
                for index, tent in enumerate(tents):
                    base = ((quarter * 2 + family) * LAGS + index) * LANES + start % LANES
                    weights_ref[group, base : base + CHUNK, :] = (coeff * tent).astype(jnp.bfloat16)


def sine_cosine(angle):
    half = 0.5 * angle
    square = half * half
    sine = cosine = 0.0
    for k in range(7, -1, -1):
        cosine = cosine * square + (-1.0) ** k / math.factorial(2 * k)
        sine = sine * square + (-1.0) ** k / math.factorial(2 * k + 1)
    sine = half * sine
    return 2.0 * sine * cosine, 1.0 - 2.0 * sine * sine


def pair_kernel(angle_ref, terms_ref, spread_ref, sums_ref, angles_ref, places_ref, even_ref, odd_ref, held_ref):
    groups, steps, lanes = sums_ref.shape
    for group in range(groups):
        for i in range(2):
            angles_ref[i, group : group + 1, :] = angle_ref[group, i : i + 1, :]
    sine, cosine = sine_cosine(angles_ref[0])
    rise, flat = sine_cosine(angles_ref[1])
    places_ref[0] = RADIUS * (cosine * flat)
    places_ref[1] = RADIUS * (sine * flat)
    places_ref[2] = RADIUS * rise
    pair = even_ref.shape[0]
    turns = groups // pair
    blocks = terms_ref.shape[0] // 2

    def places_of(turn):
        return [[places_ref[i, pl.ds(turn * pair + j, 1), :] for i in range(3)] for j in range(pair)]

    def multiply(half, weights_ref, make):
        total = None
        for part in range(PARTS):
            span = range(blocks * part // PARTS, blocks * (part + 1) // PARTS)
            terms = jnp.concatenate([terms_ref[half * blocks + k] for k in span], axis=1)
            rows = slice(span[0] * LANES, (span[-1] + 1) * LANES)
            weights = jnp.concatenate([weights_ref[j, rows, :] for j in range(pair)], axis=1)
            piece = jnp.dot(terms, weights, preferred_element_type=jnp.float32)
            total = piece if total is None else total + piece
            if part >= LEAD:
                make(part - LEAD)
        return total

    def finish(turn, total):
        total = total + held_ref[...]
        for j, place in enumerate(places_of(turn)):
            mine = total[:, j * lanes : (j + 1) * lanes]
            result = mine[3 * steps :]
            for i in range(3):
                result = result + place[i] * mine[i * steps : (i + 1) * steps]
            sums_ref[turn * pair + j] = result

    for part in range(PARTS):
        fill_weights(places_of(0), spread_ref, even_ref, 0, part)

    def body(turn, carry):
        @pl.when(turn >= 0)
        def _():
            places = places_of(turn)

            def make(part):
                fill_weights(places, spread_ref, odd_ref, 1, part)

            held_ref[...] = multiply(0, even_ref, make)
            for part in range(PARTS - LEAD, PARTS):
                make(part)

        @pl.when(turn < turns - 1)
        def _():
            places = places_of(turn + 1)

            def make(part):
                fill_weights(places, spread_ref, even_ref, 0, part)

            finish(turn, multiply(1, odd_ref, make))
            for part in range(PARTS - LEAD, PARTS):
                make(part)

        return carry

    lax.fori_loop(0, turns, body, 0)
    finish(turns - 1, multiply(1, odd_ref, lambda part: None))


def place_kernel(offset_ref, sums_ref, out_ref, later_ref, canvas_ref):
    groups, steps, lanes = sums_ref.shape
    canvas_ref[...] = jnp.zeros_like(canvas_ref)
    for block in range(groups):
        span = pl.ds(offset_ref[block], steps)
        canvas_ref[span, :] = canvas_ref[span, :] + sums_ref[block]
    out_ref[...] = canvas_ref[:steps]
    later_ref[...] = canvas_ref[steps : 2 * steps]


VMEM = pl.BlockSpec(memory_space=pltpu.VMEM)
SMEM = pl.BlockSpec(memory_space=pltpu.SMEM)
HBM = pl.BlockSpec(memory_space=pltpu.HBM)


def near_core(array):
    return pltpu.with_memory_space_constraint(array, pltpu.VMEM)


def local(flow, point_pos, area_vec, observer_angles, band_offset):
    steps = flow.shape[1]
    width = flow.shape[2]
    groups = lax.axis_size("obs")
    lanes = observer_angles.shape[1]
    times = lax.axis_size("tm")
    wide, low, high = pl.pallas_call(
        prep_kernel,
        out_shape=(
            pltpu.VMEM((groups, 2, lanes), jnp.float32),
            pltpu.VMEM((5, LAGS, width), jnp.float32),
            pltpu.VMEM((5, 1, width), jnp.float32),
        ),
        in_specs=[HBM, VMEM],
        out_specs=(VMEM,) * 3,
        scratch_shapes=[pltpu.VMEM((2, 5, ROWS, width), jnp.float32), pltpu.SemaphoreType.DMA((2,))],
        compiler_params=pltpu.CompilerParams(vmem_limit_bytes=8 << 20),
        name="prep",
    )(flow, observer_angles)
    angles = lax.all_to_all(wide, "obs", 0, 0, tiled=True)
    low = lax.ppermute(low, "tm", [(i, i + 1) for i in range(times - 1)])
    high = lax.ppermute(high, "tm", [(i + 1, i) for i in range(times - 1)])
    edge = lax.axis_index("tm").astype(jnp.int32).reshape(1)
    depth = 2 * LAGS * width
    terms, spread = pl.pallas_call(
        terms_kernel,
        out_shape=(
            pltpu.VMEM((depth // LANES, COMPS * steps, LANES), jnp.bfloat16),
            pltpu.VMEM((4, width, LANES), jnp.float32),
        ),
        in_specs=[SMEM] + [VMEM] * 5,
        out_specs=(VMEM, VMEM),
        scratch_shapes=[
            pltpu.VMEM((4, width // LANES, steps + 2 * ROWS, LANES), jnp.float32),
            pltpu.VMEM((width // LANES, 2 * COMPS, steps + ROWS, LANES), jnp.float32),
        ],
        compiler_params=pltpu.CompilerParams(vmem_limit_bytes=16 << 20),
        name="terms",
    )(edge, flow, near_core(low), near_core(high), area_vec, point_pos)
    pair = 2
    sums = pl.pallas_call(
        pair_kernel,
        out_shape=pltpu.VMEM((groups, steps, lanes), jnp.float32),
        in_specs=[VMEM] * 3,
        out_specs=VMEM,
        scratch_shapes=[
            pltpu.VMEM((2, groups, lanes), jnp.float32),
            pltpu.VMEM((3, groups, lanes), jnp.float32),
            pltpu.VMEM((pair, depth // 2, lanes), jnp.bfloat16),
            pltpu.VMEM((pair, depth // 2, lanes), jnp.bfloat16),
            pltpu.VMEM((COMPS * steps, pair * lanes), jnp.float32),
        ],
        compiler_params=pltpu.CompilerParams(vmem_limit_bytes=24 << 20),
        name="pairs",
    )(near_core(angles), near_core(terms), near_core(spread))
    sums = lax.all_to_all(sums, "obs", 0, 0, tiled=True)
    offsets = lax.dynamic_index_in_dim(band_offset, lax.axis_index("obs"), 0, keepdims=False)
    out, later = pl.pallas_call(
        place_kernel,
        out_shape=(pltpu.VMEM((steps, lanes), jnp.float32),) * 2,
        in_specs=[SMEM, VMEM],
        out_specs=(VMEM, VMEM),
        scratch_shapes=[pltpu.VMEM((2 * steps, lanes), jnp.float32)],
        compiler_params=pltpu.CompilerParams(vmem_limit_bytes=8 << 20),
        name="place",
    )(offsets, near_core(sums))
    carried = lax.ppermute(later, "tm", [(i, i + 1) for i in range(times - 1)])
    return out + carried


def solution(mesh):
    in_specs = (P(None, "tm", "obs"), P(None, "obs"), P(None, "obs"), P(None, "obs"), P())
    out_specs = P("tm", "obs")
    return jax.shard_map(local, mesh=mesh, in_specs=in_specs, out_specs=out_specs, check_vma=False)
```

time: 65.6 us -> 58.9 us (0.90)
  Pallas kernels: 17.6 us -> 12.8 us
  local copies, waits for them, and re-layouts: 5.7 us -> 4.27 us
  other arithmetic: 1.38 us -> 0.62 us
    pallas_call x3 -> x4, Pallas kernels: 17.6 us -> 12.8 us  [the longest x1 10.5 us: local(): pl.pallas_call(pair_kernel, out_shape=pltpu.VMEM((groups, steps, lanes),...]
    unnamed x10 -> x12, local copies, waits for them, and re-layouts: 2.02 us -> 4.26 us
    slice x2 -> x0, local copies, waits for them, and re-layouts: 1.81 us -> none  [the longest x1 0.91 us: local(): flow[:, steps - LAGS:]]
    broadcast_in_dim x1 -> x0, local copies, waits for them, and re-layouts: 1.29 us -> none  [local(): jnp.broadcast_to(observer_angles[None], (groups, 2, lanes))]
    add x1, other arithmetic: 1.38 us -> 0.62 us  [local(): return out + carried]
  transfers between devices with their start and end apart: 5 -> 5, of which waited for: 3 -> 3; matrix products, arithmetic and copies ran while one was open for 4% -> 0% of each run, Pallas kernels for 6% -> 2%
where the time goes in v2:
time: 58.9 us; the launch traced here: 58.4 us
  starting transfers between devices  22.4 us (38%)
  waiting for transfers between devices  18.3 us (31%)
  Pallas kernels  12.8 us (22%)
  local copies, waits for them, and re-layouts  4.27 us (7%)
  other arithmetic  0.62 us (1%)
    all_to_all x1, waiting for transfers between devices, local(): sums = lax.all_to_all(sums, 'obs', 0, 0, tiled=True)  12.4 us
    pallas_call x1, Pallas kernels, local(): pl.pallas_call(pair_kernel, out_shape=pltpu.VMEM((groups, steps, lanes),...  10.5 us
    all_to_all x1, starting transfers between devices, local(): angles = lax.all_to_all(wide, 'obs', 0, 0, tiled=True)  7.05 us
    all_to_all x1, starting transfers between devices, local(): sums = lax.all_to_all(sums, 'obs', 0, 0, tiled=True)  6.92 us
    ppermute x1, starting transfers between devices, local(): high = lax.ppermute(high, 'tm', [(i + 1, i) for i in range(times - 1)])  4.57 us
    ppermute x1, waiting for transfers between devices, local(): carried = lax.ppermute(later, 'tm', [(i, i + 1) for i in range(times - 1)])  4.52 us
    unnamed x12, local copies, waits for them, and re-layouts  4.26 us
    ppermute x1, starting transfers between devices, local(): low = lax.ppermute(low, 'tm', [(i, i + 1) for i in range(times - 1)])  1.92 us
  transfers between devices with their start and end apart: 5, of which 3 were waited for; matrix products, arithmetic and copies ran while one was open for 0% of the time, Pallas kernels for 2%

profile of v2, /device:TPU:128, one launch (start us, length us, event | category | flops | bytes accessed | tf_op | source)
XLA Modules:
  0.0 58.4 jit_solution(18192119480876447215)
XLA Ops:
  0.0 0.0 copy-start
  0.0 0.0 copy-start.1
  0.0 1.1 %copy-done.1 = f32[5,64,512]{2,1,0:T(8,128)S(1)} copy-done((f32[5,64,512]{2,1,0:T(8,128)S(1)}, f32[5,64,512]{2,1,0:T(8,128)}, u32[]{:S(2)}) %copy-start.1) | copy-done | bytes 655384
  1.1 0.0 copy-start.5
  1.1 0.7 %copy-done.5 = f32[2,128]{1,0:T(2,128)S(1)} copy-done((f32[2,128]{1,0:T(2,128)S(1)}, f32[2,128]{1,0:T(2,128)}, u32[]{:S(2)}) %copy-start.5) | copy-done | bytes 1048
  1.8 0.7 %prep.1 = (f32[16,2,128]{2,1,0:T(2,128)}, f32[5,4,512]{2,1,0:T(4,128)S(1)}, f32[5,1,512]{2,1,0:T(1,128)S(1)}) custom-call(f32[5,64,512]{2,1,0:T(8,128)S(1)} %copy-done.1, f32[2,128]{1,0:T(2,128)S(1)} %copy-done.5), custom_call_target="tpu_custom_call" | custom-call | tf_op jit(solution)/shard_map/prep/pallas_call | solution.py:225
  2.5 1.9 %collective-permute-start = (f32[5,4,512]{2,1,0:T(4,128)S(1)}, f32[5,4,512]{2,1,0:T(4,128)S(1)}, u32[]{:S(2)}, u32[]{:S(2)}) collective-permute-start(f32[5,4,512]{2,1,0:T(4,128)S(1)} %get-tuple-element.13), channel_id=1, source_target_pairs={{0,1},{1,2},{2,3},{3,4},{4,5},{5,6},{6,7},{7,8},{8,9},{9,10},{10,1... | collective-permute-start | bytes 122888 | tf_op jit(solution)/shard_map/ppermute | solution.py:239
  4.4 7.0 %all-to-all-start = ((f32[16,2,128]{2,1,0:T(2,128)}), f32[16,2,128]{2,1,0:T(2,128)S(1)}, u32[]{:S(2)}, u32[]{:S(2)}) async-start(f32[16,2,128]{2,1,0:T(2,128)} %get-tuple-element.12), calls=%async_computation | async-start | bytes 32768 | tf_op jit(solution)/shard_map/all_to_all | solution.py:238
  11.4 4.6 %collective-permute-start.1 = (f32[5,1,512]{2,1,0:T(1,128)S(1)}, f32[5,1,512]{2,1,0:T(1,128)S(1)}, u32[]{:S(2)}, u32[]{:S(2)}) collective-permute-start(f32[5,1,512]{2,1,0:T(1,128)S(1)} %get-tuple-element.14), channel_id=1, source_target_pairs={{1,0},{2,1},{3,2},{4,3},{5,4},{6,5},{7,6},{8,7},{9,8},{10,9},{11,1... | collective-permute-start | bytes 30728 | tf_op jit(solution)/shard_map/ppermute | solution.py:240
  16.0 1.4 %collective-permute-done.1.high_ref = f32[5,1,512]{2,1,0:T(1,128)S(1)} collective-permute-done((f32[5,1,512]{2,1,0:T(1,128)S(1)}, f32[5,1,512]{2,1,0:T(1,128)S(1)}, u32[]{:S(2)}, u32[]{:S(2)}) %collective-permute-start.1) | collective-permute-done | bytes 10272 | tf_op jit(solution)/shard_map/ppermute | solution.py:240
  17.4 0.0 collective-permute-done.low_ref
  17.4 0.0 copy-start.2
  17.4 1.1 %copy-done.2 = f32[5,64,512]{2,1,0:T(8,128)S(1)} copy-done((f32[5,64,512]{2,1,0:T(8,128)S(1)}, f32[5,64,512]{2,1,0:T(8,128)}, u32[]{:S(2)}) %copy-start.2) | copy-done | bytes 655384
  18.5 0.0 copy-start.3
  18.5 0.7 %copy-done.3 = f32[3,512]{1,0:T(4,128)S(1)} copy-done((f32[3,512]{1,0:T(4,128)S(1)}, f32[3,512]{1,0:T(4,128)}, u32[]{:S(2)}) %copy-start.3) | copy-done | bytes 6168
  19.2 0.0 copy-start.4
  19.2 0.7 %copy-done.4 = f32[3,512]{1,0:T(4,128)S(1)} copy-done((f32[3,512]{1,0:T(4,128)S(1)}, f32[3,512]{1,0:T(4,128)}, u32[]{:S(2)}) %copy-start.4) | copy-done | bytes 6168
  19.9 0.9 %terms.1 = (bf16[32,256,128]{2,1,0:T(8,128)(2,1)S(1)}, f32[4,512,128]{2,1,0:T(8,128)S(1)}) custom-call(s32[1]{0:T(128)} %bitcast.1.edge_ref, f32[5,64,512]{2,1,0:T(8,128)S(1)} %copy-done.2, f32[5,4,512]{2,1,0:T(4,128)S(1)} %collective-permute-done.low_ref, f32[5,1,512]{2,1,0:T(1,128)S(1)} %collective-permute-done.1.high_ref, f32[3,512]{1,0:T(4,128)S(1)} %copy-done.3, ...), custom_call_target="tpu_custom_call" | custom-call | tf_op jit(solution)/shard_map/terms/pallas_call | solution.py:243
  20.8 0.0 all-to-all-done.angle_ref
  20.8 10.5 %pairs.1 = f32[16,64,128]{2,1,0:T(8,128)} custom-call(f32[16,2,128]{2,1,0:T(2,128)S(1)} %all-to-all-done.angle_ref, bf16[32,256,128]{2,1,0:T(8,128)(2,1)S(1)} %get-tuple-element.15.terms_ref, f32[4,512,128]{2,1,0:T(8,128)S(1)} %get-tuple-element.16.spread_ref), custom_call_target="tpu_custom_call" | custom-call | tf_op jit(solution)/shard_map/pairs/pallas_call | solution.py:259
  31.3 6.9 %all-to-all-start.1 = ((f32[16,64,128]{2,1,0:T(8,128)}), f32[16,64,128]{2,1,0:T(8,128)S(1)}, u32[]{:S(2)}, u32[]{:S(2)}) async-start(f32[16,64,128]{2,1,0:T(8,128)} %pairs.1), calls=%async_computation.1 | async-start | bytes 1048576 | tf_op jit(solution)/shard_map/all_to_all | solution.py:274
  38.2 0.0 copy-done
  38.3 12.4 %all-to-all-done.1.sums_ref = f32[16,64,128]{2,1,0:T(8,128)S(1)} async-done(((f32[16,64,128]{2,1,0:T(8,128)}), f32[16,64,128]{2,1,0:T(8,128)S(1)}, u32[]{:S(2)}, u32[]{:S(2)}) %all-to-all-start.1) | async-done | bytes 524320 | tf_op jit(solution)/shard_map/all_to_all | solution.py:274
  50.7 0.7 %place.1 = (f32[64,128]{1,0:T(8,128)S(1)}, f32[64,128]{1,0:T(8,128)S(1)}) custom-call(s32[16]{0:T(128)S(1)} %dynamic-slice_bitcast_fusion.offset_ref, f32[16,64,128]{2,1,0:T(8,128)S(1)} %all-to-all-done.1.sums_ref), custom_call_target="tpu_custom_call" | custom-call | tf_op jit(solution)/shard_map/place/pallas_call | solution.py:276
  51.4 1.9 %collective-permute-start.2 = (f32[64,128]{1,0:T(8,128)S(1)}, f32[64,128]{1,0:T(8,128)S(1)}, u32[]{:S(2)}, u32[]{:S(2)}) collective-permute-start(f32[64,128]{1,0:T(8,128)S(1)} %get-tuple-element.18), channel_id=1, source_target_pairs={{0,1},{1,2},{2,3},{3,4},{4,5},{5,6},{6,7},{7,8},{8,9},{9,10},{10,1... | collective-permute-start | bytes 98312 | tf_op jit(solution)/shard_map/ppermute | solution.py:285
  53.3 4.5 %collective-permute-done.2 = f32[64,128]{1,0:T(8,128)S(1)} collective-permute-done((f32[64,128]{1,0:T(8,128)S(1)}, f32[64,128]{1,0:T(8,128)S(1)}, u32[]{:S(2)}, u32[]{:S(2)}) %collective-permute-start.2) | collective-permute-done | bytes 32800 | tf_op jit(solution)/shard_map/ppermute | solution.py:285
  57.8 0.6 %add.8 = f32[64,128]{1,0:T(8,128)} add(f32[64,128]{1,0:T(8,128)S(1)} %get-tuple-element.17, f32[64,128]{1,0:T(8,128)S(1)} %collective-permute-done.2) | non-fusion elementwise | flops 8192 | bytes 98304 | tf_op jit(solution)/shard_map/add | solution.py:286
  (1 shorter events, 0.0 us)
Async XLA Ops:
  0.0 38.2 %copy-start = (s32[16,16]{1,0:T(8,128)S(1)}, s32[16,16]{1,0:T(8,128)}, u32[]{:S(2)}) copy-start(s32[16,16]{1,0:T(8,128)} %param.9) | copy-start | bytes 3076
  0.0 1.1 %copy-start.1 = (f32[5,64,512]{2,1,0:T(8,128)S(1)}, f32[5,64,512]{2,1,0:T(8,128)}, u32[]{:S(2)}) copy-start(f32[5,64,512]{2,1,0:T(8,128)} %flow_ref.3) | copy-start | bytes 1966084
  1.1 0.7 %copy-start.5 = (f32[2,128]{1,0:T(2,128)S(1)}, f32[2,128]{1,0:T(2,128)}, u32[]{:S(2)}) copy-start(f32[2,128]{1,0:T(2,128)} %angle_ref.1) | copy-start | bytes 3076
  2.5 14.9 %collective-permute-start = (f32[5,4,512]{2,1,0:T(4,128)S(1)}, f32[5,4,512]{2,1,0:T(4,128)S(1)}, u32[]{:S(2)}, u32[]{:S(2)}) collective-permute-start(f32[5,4,512]{2,1,0:T(4,128)S(1)} %get-tuple-element.13), channel_id=1, source_target_pairs={{0,1},{1,2},{2,3},{3,4},{4,5},{5,6},{6,7},{7,8},{8,9},{9,10},{10,1... | collective-permute-start | bytes 122888 | tf_op jit(solution)/shard_map/ppermute | solution.py:239
  4.4 16.4 %all-to-all-start = ((f32[16,2,128]{2,1,0:T(2,128)}), f32[16,2,128]{2,1,0:T(2,128)S(1)}, u32[]{:S(2)}, u32[]{:S(2)}) async-start(f32[16,2,128]{2,1,0:T(2,128)} %get-tuple-element.12), calls=%async_computation | async-start | bytes 32768 | tf_op jit(solution)/shard_map/all_to_all | solution.py:238
  11.4 5.9 %collective-permute-start.1 = (f32[5,1,512]{2,1,0:T(1,128)S(1)}, f32[5,1,512]{2,1,0:T(1,128)S(1)}, u32[]{:S(2)}, u32[]{:S(2)}) collective-permute-start(f32[5,1,512]{2,1,0:T(1,128)S(1)} %get-tuple-element.14), channel_id=1, source_target_pairs={{1,0},{2,1},{3,2},{4,3},{5,4},{6,5},{7,6},{8,7},{9,8},{10,9},{11,1... | collective-permute-start | bytes 30728 | tf_op jit(solution)/shard_map/ppermute | solution.py:240
  17.4 1.1 %copy-start.2 = (f32[5,64,512]{2,1,0:T(8,128)S(1)}, f32[5,64,512]{2,1,0:T(8,128)}, u32[]{:S(2)}) copy-start(f32[5,64,512]{2,1,0:T(8,128)} %flow_ref.3) | copy-start | bytes 1966084
  18.5 0.7 %copy-start.3 = (f32[3,512]{1,0:T(4,128)S(1)}, f32[3,512]{1,0:T(4,128)}, u32[]{:S(2)}) copy-start(f32[3,512]{1,0:T(4,128)} %area_ref.1) | copy-start | bytes 18436
  19.2 0.7 %copy-start.4 = (f32[3,512]{1,0:T(4,128)S(1)}, f32[3,512]{1,0:T(4,128)}, u32[]{:S(2)}) copy-start(f32[3,512]{1,0:T(4,128)} %point_ref.1) | copy-start | bytes 18436
  31.3 19.4 %all-to-all-start.1 = ((f32[16,64,128]{2,1,0:T(8,128)}), f32[16,64,128]{2,1,0:T(8,128)S(1)}, u32[]{:S(2)}, u32[]{:S(2)}) async-start(f32[16,64,128]{2,1,0:T(8,128)} %pairs.1), calls=%async_computation.1 | async-start | bytes 1048576 | tf_op jit(solution)/shard_map/all_to_all | solution.py:274
  51.4 6.4 %collective-permute-start.2 = (f32[64,128]{1,0:T(8,128)S(1)}, f32[64,128]{1,0:T(8,128)S(1)}, u32[]{:S(2)}, u32[]{:S(2)}) collective-permute-start(f32[64,128]{1,0:T(8,128)S(1)} %get-tuple-element.18), channel_id=1, source_target_pairs={{0,1},{1,2},{2,3},{3,4},{4,5},{5,6},{6,7},{7,8},{8,9},{9,10},{10,1... | collective-permute-start | bytes 98312 | tf_op jit(solution)/shard_map/ppermute | solution.py:285

commit v3 on v2

--- a/solution.py
+++ b/solution.py
@@ -6,6 +6,7 @@
 from jax.experimental import pallas as pl
 from jax.experimental.pallas import tpu as pltpu
 from jax.sharding import PartitionSpec as P
+
 
 LAGS = 4
 NEAR_RANGE = 3.25
@@ -17,8 +18,7 @@
 ROWS = 8
 LANES = 128
 CHUNK = 16
-PARTS = 8
-LEAD = 0
+PARTS = 16
 
 
 def prep_kernel(flow_ref, angle_ref, wide_ref, low_ref, high_ref, edges_ref, sem):
@@ -27,23 +27,26 @@
         pltpu.make_async_copy(flow_ref.at[:, pl.ds(start, ROWS), :], edges_ref.at[side], sem.at[side])
         for side, start in enumerate((steps - ROWS, 0))
     ]
+    copies += [
+        pltpu.make_async_copy(angle_ref, wide_ref.at[group], sem.at[2 + group]) for group in range(wide_ref.shape[0])
+    ]
     for copy in copies:
         copy.start()
-    for group in range(wide_ref.shape[0]):
-        wide_ref[group] = angle_ref[...]
-    for copy in copies:
+    for copy in copies[:2]:
         copy.wait()
     low_ref[...] = edges_ref[0, :, ROWS - LAGS :, :]
     high_ref[...] = edges_ref[1, :, :1, :]
-
-
-def terms_kernel(edge_ref, flow_ref, low_ref, high_ref, area_ref, point_ref, terms_ref, spread_ref, field_ref, part_ref):
+    for copy in copies[2:]:
+        copy.wait()
+
+
+def terms_kernel(edge_ref, own_ref, flow_ref, low_ref, high_ref, area_ref, point_ref, terms_ref, spread_ref, field_ref, part_ref):
     steps = flow_ref.shape[1]
     width = flow_ref.shape[2]
     count = steps + ROWS
     for cut in range(width // LANES):
         lanes = slice(cut * LANES, (cut + 1) * LANES)
-        area = [SCALE * area_ref[i : i + 1, lanes] for i in range(3)]
+        area = [area_ref[i : i + 1, lanes] for i in range(3)]
         point = [(1.0 / SOUND_STEP) * point_ref[i : i + 1, lanes] for i in range(3)]
 
         def fields(source, start, rows):
@@ -92,10 +95,10 @@
             spread_ref[i, lanes, :] = jnp.broadcast_to(turned[:, i : i + 1], (LANES, LANES))
 
 
-def fill_weights(places, spread_ref, weights_ref, half, part):
-    span = spread_ref.shape[1] // 2
+def fill_weights(places, spread_ref, weights_ref, part):
+    span = spread_ref.shape[1]
     for start in range(span * part // PARTS, span * (part + 1) // PARTS, CHUNK):
-        rows = slice(half * span + start, half * span + start + CHUNK)
+        rows = slice(start, start + CHUNK)
         spread = [spread_ref[i, rows, :] for i in range(4)]
         for group, place in enumerate(places):
             square = spread[3] - place[0] * spread[0] - place[1] * spread[1] - place[2] * spread[2]
@@ -126,7 +129,7 @@
     return 2.0 * sine * cosine, 1.0 - 2.0 * sine * sine
 
 
-def pair_kernel(angle_ref, terms_ref, spread_ref, sums_ref, angles_ref, places_ref, even_ref, odd_ref, held_ref):
+def pair_kernel(angle_ref, terms_ref, spread_ref, sums_ref, angles_ref, places_ref, even_ref, odd_ref, held_ref, rest_ref):
     groups, steps, lanes = sums_ref.shape
     for group in range(groups):
         for i in range(2):
@@ -138,70 +141,63 @@
     places_ref[2] = RADIUS * rise
     pair = even_ref.shape[0]
     turns = groups // pair
-    blocks = terms_ref.shape[0] // 2
+    blocks = terms_ref.shape[0]
 
     def places_of(turn):
         return [[places_ref[i, pl.ds(turn * pair + j, 1), :] for i in range(3)] for j in range(pair)]
 
-    def multiply(half, weights_ref, make):
+    def multiply(weights_ref, make):
         total = None
         for part in range(PARTS):
             span = range(blocks * part // PARTS, blocks * (part + 1) // PARTS)
-            terms = jnp.concatenate([terms_ref[half * blocks + k] for k in span], axis=1)
+            terms = jnp.concatenate([terms_ref[k] for k in span], axis=1)
             rows = slice(span[0] * LANES, (span[-1] + 1) * LANES)
             weights = jnp.concatenate([weights_ref[j, rows, :] for j in range(pair)], axis=1)
             piece = jnp.dot(terms, weights, preferred_element_type=jnp.float32)
             total = piece if total is None else total + piece
-            if part >= LEAD:
-                make(part - LEAD)
+            make(part)
         return total
 
-    def finish(turn, total):
-        total = total + held_ref[...]
+    def finish(turn, total_ref):
         for j, place in enumerate(places_of(turn)):
-            mine = total[:, j * lanes : (j + 1) * lanes]
+            mine = total_ref[:, j * lanes : (j + 1) * lanes]
             result = mine[3 * steps :]
             for i in range(3):
                 result = result + place[i] * mine[i * steps : (i + 1) * steps]
-            sums_ref[turn * pair + j] = result
+            sums_ref[turn * pair + j] = SCALE * result
 
     for part in range(PARTS):
-        fill_weights(places_of(0), spread_ref, even_ref, 0, part)
-
-    def body(turn, carry):
-        @pl.when(turn >= 0)
+        fill_weights(places_of(0), spread_ref, even_ref, part)
+
+    def body(step, carry):
+        even = 2 * step
+        odd = 2 * step + 1
+
+        @pl.when(step >= 0)
         def _():
-            places = places_of(turn)
-
-            def make(part):
-                fill_weights(places, spread_ref, odd_ref, 1, part)
-
-            held_ref[...] = multiply(0, even_ref, make)
-            for part in range(PARTS - LEAD, PARTS):
-                make(part)
-
-        @pl.when(turn < turns - 1)
+            finish(jnp.maximum(even - 1, 0), rest_ref)
+            places = places_of(odd)
+            held_ref[...] = multiply(even_ref, lambda part: fill_weights(places, spread_ref, odd_ref, part))
+
+        @pl.when(odd < turns - 1)
         def _():
-            places = places_of(turn + 1)
-
-            def make(part):
-                fill_weights(places, spread_ref, even_ref, 0, part)
-
-            finish(turn, multiply(1, odd_ref, make))
-            for part in range(PARTS - LEAD, PARTS):
-                make(part)
+            finish(even, held_ref)
+            places = places_of(odd + 1)
+            rest_ref[...] = multiply(odd_ref, lambda part: fill_weights(places, spread_ref, even_ref, part))
 
         return carry
 
-    lax.fori_loop(0, turns, body, 0)
-    finish(turns - 1, multiply(1, odd_ref, lambda part: None))
-
-
-def place_kernel(offset_ref, sums_ref, out_ref, later_ref, canvas_ref):
-    groups, steps, lanes = sums_ref.shape
+    lax.fori_loop(0, turns // 2, body, 0)
+    finish(turns - 2, held_ref)
+    rest_ref[...] = multiply(odd_ref, lambda part: None)
+    finish(turns - 1, rest_ref)
+
+
+def place_kernel(own_ref, offset_ref, sums_ref, out_ref, later_ref, canvas_ref):
+    groups, steps, _ = sums_ref.shape
     canvas_ref[...] = jnp.zeros_like(canvas_ref)
     for block in range(groups):
-        span = pl.ds(offset_ref[block], steps)
+        span = pl.ds(offset_ref[own_ref[0], block], steps)
         canvas_ref[span, :] = canvas_ref[span, :] + sums_ref[block]
     out_ref[...] = canvas_ref[:steps]
     later_ref[...] = canvas_ref[steps : 2 * steps]
@@ -214,6 +210,10 @@
 
 def near_core(array):
     return pltpu.with_memory_space_constraint(array, pltpu.VMEM)
+
+
+def in_hbm(array):
+    return pltpu.with_memory_space_constraint(array, pltpu.HBM)
 
 
 def local(flow, point_pos, area_vec, observer_angles, band_offset):
@@ -225,20 +225,21 @@
     wide, low, high = pl.pallas_call(
         prep_kernel,
         out_shape=(
-            pltpu.VMEM((groups, 2, lanes), jnp.float32),
+            jax.ShapeDtypeStruct((groups, 2, lanes), jnp.float32),
             pltpu.VMEM((5, LAGS, width), jnp.float32),
             pltpu.VMEM((5, 1, width), jnp.float32),
         ),
-        in_specs=[HBM, VMEM],
-        out_specs=(VMEM,) * 3,
-        scratch_shapes=[pltpu.VMEM((2, 5, ROWS, width), jnp.float32), pltpu.SemaphoreType.DMA((2,))],
+        in_specs=[HBM, HBM],
+        out_specs=(HBM, VMEM, VMEM),
+        scratch_shapes=[pltpu.VMEM((2, 5, ROWS, width), jnp.float32), pltpu.SemaphoreType.DMA((2 + groups,))],
         compiler_params=pltpu.CompilerParams(vmem_limit_bytes=8 << 20),
         name="prep",
-    )(flow, observer_angles)
+    )(in_hbm(flow), in_hbm(observer_angles))
     angles = lax.all_to_all(wide, "obs", 0, 0, tiled=True)
     low = lax.ppermute(low, "tm", [(i, i + 1) for i in range(times - 1)])
     high = lax.ppermute(high, "tm", [(i + 1, i) for i in range(times - 1)])
     edge = lax.axis_index("tm").astype(jnp.int32).reshape(1)
+    own = lax.axis_index("obs").astype(jnp.int32).reshape(1)
     depth = 2 * LAGS * width
     terms, spread = pl.pallas_call(
         terms_kernel,
@@ -246,7 +247,7 @@
             pltpu.VMEM((depth // LANES, COMPS * steps, LANES), jnp.bfloat16),
             pltpu.VMEM((4, width, LANES), jnp.float32),
         ),
-        in_specs=[SMEM] + [VMEM] * 5,
+        in_specs=[SMEM] * 2 + [VMEM] * 5,
         out_specs=(VMEM, VMEM),
         scratch_shapes=[
             pltpu.VMEM((4, width // LANES, steps + 2 * ROWS, LANES), jnp.float32),
@@ -254,7 +255,7 @@
         ],
         compiler_params=pltpu.CompilerParams(vmem_limit_bytes=16 << 20),
         name="terms",
-    )(edge, flow, near_core(low), near_core(high), area_vec, point_pos)
+    )(edge, own, in_hbm(flow), near_core(low), near_core(high), in_hbm(area_vec), in_hbm(point_pos))
     pair = 2
     sums = pl.pallas_call(
         pair_kernel,
@@ -264,24 +265,24 @@
         scratch_shapes=[
             pltpu.VMEM((2, groups, lanes), jnp.float32),
             pltpu.VMEM((3, groups, lanes), jnp.float32),
-            pltpu.VMEM((pair, depth // 2, lanes), jnp.bfloat16),
-            pltpu.VMEM((pair, depth // 2, lanes), jnp.bfloat16),
+            pltpu.VMEM((pair, depth, lanes), jnp.bfloat16),
+            pltpu.VMEM((pair, depth, lanes), jnp.bfloat16),
+            pltpu.VMEM((COMPS * steps, pair * lanes), jnp.float32),
             pltpu.VMEM((COMPS * steps, pair * lanes), jnp.float32),
         ],
         compiler_params=pltpu.CompilerParams(vmem_limit_bytes=24 << 20),
         name="pairs",
     )(near_core(angles), near_core(terms), near_core(spread))
     sums = lax.all_to_all(sums, "obs", 0, 0, tiled=True)
-    offsets = lax.dynamic_index_in_dim(band_offset, lax.axis_index("obs"), 0, keepdims=False)
     out, later = pl.pallas_call(
         place_kernel,
         out_shape=(pltpu.VMEM((steps, lanes), jnp.float32),) * 2,
-        in_specs=[SMEM, VMEM],
+        in_specs=[SMEM, SMEM, VMEM],
         out_specs=(VMEM, VMEM),
         scratch_shapes=[pltpu.VMEM((2 * steps, lanes), jnp.float32)],
         compiler_params=pltpu.CompilerParams(vmem_limit_bytes=8 << 20),
         name="place",
-    )(offsets, near_core(sums))
+    )(own, band_offset, near_core(sums))
     carried = lax.ppermute(later, "tm", [(i, i + 1) for i in range(times - 1)])
     return out + carried
 

time: 58.9 us -> 53.1 us (0.902)
  blocking collectives: 0 us -> 19.2 us
  waiting for transfers between devices: 18.3 us -> 5.88 us
  starting transfers between devices: 22.4 us -> 15.5 us
  local copies, waits for them, and re-layouts: 4.27 us -> 0.01 us
  Pallas kernels: 12.8 us -> 11.6 us
    all_to_all x0 -> x1, blocking collectives: none -> 19.2 us  [local(): sums = lax.all_to_all(sums, 'obs', 0, 0, tiled=True)]
    all_to_all x1 -> x0, waiting for transfers between devices: 12.4 us -> none  [local(): sums = lax.all_to_all(sums, 'obs', 0, 0, tiled=True)]
    all_to_all x1 -> x0, starting transfers between devices: 6.92 us -> none  [local(): sums = lax.all_to_all(sums, 'obs', 0, 0, tiled=True)]
    unnamed x12 -> x2, local copies, waits for them, and re-layouts: 4.26 us -> 0.01 us
    pallas_call x1, Pallas kernels: 10.5 us -> 6.85 us  [local(): pl.pallas_call(pair_kernel, out_shape=pltpu.VMEM((groups, steps, lanes),...]
    pallas_call x1, Pallas kernels: 0.66 us -> 1.82 us  [local(): pl.pallas_call(prep_kernel, out_shape=(jax.ShapeDtypeStruct((groups, 2, l...]
    pallas_call x1, Pallas kernels: 0.93 us -> 2.08 us  [local(): pl.pallas_call(terms_kernel, out_shape=(pltpu.VMEM((depth // LANES, COMPS...]
  transfers between devices with their start and end apart: 5 -> 4, of which waited for: 3 -> 2; matrix products, arithmetic and copies ran while one was open for 0% -> 0% of each run, Pallas kernels for 2% -> 4%
where the time goes in v3:
time: 53.1 us; the launch traced here: 52.8 us
  blocking collectives  19.2 us (36%)
  starting transfers between devices  15.5 us (29%)
  Pallas kernels  11.6 us (22%)
  waiting for transfers between devices  5.88 us (11%)
  other arithmetic  0.62 us (1%)
    all_to_all x1, blocking collectives, local(): sums = lax.all_to_all(sums, 'obs', 0, 0, tiled=True)  19.2 us
    all_to_all x1, starting transfers between devices, local(): angles = lax.all_to_all(wide, 'obs', 0, 0, tiled=True)  7.05 us
    pallas_call x1, Pallas kernels, local(): pl.pallas_call(pair_kernel, out_shape=pltpu.VMEM((groups, steps, lanes),...  6.85 us
    ppermute x1, starting transfers between devices, local(): high = lax.ppermute(high, 'tm', [(i + 1, i) for i in range(times - 1)])  4.57 us
    ppermute x1, waiting for transfers between devices, local(): carried = lax.ppermute(later, 'tm', [(i, i + 1) for i in range(times - 1)])  4.52 us
    pallas_call x1, Pallas kernels, local(): pl.pallas_call(terms_kernel, out_shape=(pltpu.VMEM((depth // LANES, COMPS...  2.08 us
    ppermute x1, starting transfers between devices, local(): low = lax.ppermute(low, 'tm', [(i, i + 1) for i in range(times - 1)])  1.92 us
    ppermute x1, starting transfers between devices, local(): carried = lax.ppermute(later, 'tm', [(i, i + 1) for i in range(times - 1)])  1.92 us
  transfers between devices with their start and end apart: 4, of which 2 were waited for; matrix products, arithmetic and copies ran while one was open for 0% of the time, Pallas kernels for 4%

profile of v3, /device:TPU:128, one launch (start us, length us, event | category | flops | bytes accessed | tf_op | source)
XLA Modules:
  0.0 52.8 jit_solution(17240482599265332884)
XLA Ops:
  0.0 1.8 %prep.1 = (f32[16,2,128]{2,1,0:T(2,128)}, f32[5,4,512]{2,1,0:T(4,128)S(1)}, f32[5,1,512]{2,1,0:T(1,128)S(1)}) custom-call(f32[5,64,512]{2,1,0:T(8,128)} %flow_ref.3, f32[2,128]{1,0:T(2,128)} %angle_ref.1), custom_call_target="tpu_custom_call" | custom-call | tf_op jit(solution)/shard_map/prep/pallas_call | solution.py:225
  1.8 1.9 %collective-permute-start = (f32[5,4,512]{2,1,0:T(4,128)S(1)}, f32[5,4,512]{2,1,0:T(4,128)S(1)}, u32[]{:S(2)}, u32[]{:S(2)}) collective-permute-start(f32[5,4,512]{2,1,0:T(4,128)S(1)} %get-tuple-element.13), channel_id=1, source_target_pairs={{0,1},{1,2},{2,3},{3,4},{4,5},{5,6},{6,7},{7,8},{8,9},{9,10},{10,1... | collective-permute-start | bytes 122888 | tf_op jit(solution)/shard_map/ppermute | solution.py:239
  3.8 7.0 %all-to-all-start = ((f32[16,2,128]{2,1,0:T(2,128)}), f32[16,2,128]{2,1,0:T(2,128)S(1)}, u32[]{:S(2)}, u32[]{:S(2)}) async-start(f32[16,2,128]{2,1,0:T(2,128)} %get-tuple-element.12), calls=%async_computation | async-start | bytes 32768 | tf_op jit(solution)/shard_map/all_to_all | solution.py:238
  10.8 4.6 %collective-permute-start.1 = (f32[5,1,512]{2,1,0:T(1,128)S(1)}, f32[5,1,512]{2,1,0:T(1,128)S(1)}, u32[]{:S(2)}, u32[]{:S(2)}) collective-permute-start(f32[5,1,512]{2,1,0:T(1,128)S(1)} %get-tuple-element.14), channel_id=1, source_target_pairs={{1,0},{2,1},{3,2},{4,3},{5,4},{6,5},{7,6},{8,7},{9,8},{10,9},{11,1... | collective-permute-start | bytes 30728 | tf_op jit(solution)/shard_map/ppermute | solution.py:240
  15.4 1.4 %collective-permute-done.1.high_ref = f32[5,1,512]{2,1,0:T(1,128)S(1)} collective-permute-done((f32[5,1,512]{2,1,0:T(1,128)S(1)}, f32[5,1,512]{2,1,0:T(1,128)S(1)}, u32[]{:S(2)}, u32[]{:S(2)}) %collective-permute-start.1) | collective-permute-done | bytes 10272 | tf_op jit(solution)/shard_map/ppermute | solution.py:240
  16.8 0.0 collective-permute-done.low_ref
  16.8 2.1 %terms.1 = (bf16[32,256,128]{2,1,0:T(8,128)(2,1)S(1)}, f32[4,512,128]{2,1,0:T(8,128)S(1)}) custom-call(s32[1]{0:T(128)} %bitcast.1.edge_ref, s32[1]{0:T(128)} %bitcast.own_ref, f32[5,64,512]{2,1,0:T(8,128)} %flow_ref.3, f32[5,4,512]{2,1,0:T(4,128)S(1)} %collective-permute-done.low_ref, f32[5,1,512]{2,1,0:T(1,128)S(1)} %collective-permute-done.1.high_ref, ...), custom_call_target="tpu_custom_call" | custom-call | tf_op jit(solution)/shard_map/terms/pallas_call | solution.py:244
  18.8 0.0 all-to-all-done.angle_ref
  18.9 0.0 copy-start
  18.9 6.9 %pairs.1 = f32[16,64,128]{2,1,0:T(8,128)S(1)} custom-call(f32[16,2,128]{2,1,0:T(2,128)S(1)} %all-to-all-done.angle_ref, bf16[32,256,128]{2,1,0:T(8,128)(2,1)S(1)} %get-tuple-element.15.terms_ref, f32[4,512,128]{2,1,0:T(8,128)S(1)} %get-tuple-element.16.spread_ref), custom_call_target="tpu_custom_call" | custom-call | tf_op jit(solution)/shard_map/pairs/pallas_call | solution.py:260
  25.7 19.2 %all_to_all.10.sums_ref = f32[16,64,128]{2,1,0:T(8,128)S(1)} all-to-all(f32[16,64,128]{2,1,0:T(8,128)S(1)} %pairs.1), channel_id=1, replica_groups=mesh['obs'=16,'tm'=32] {'obs'}, dimensions={0} | all-to-all | bytes 1048576 | tf_op jit(solution)/shard_map/all_to_all | solution.py:276
  44.9 0.0 copy-done
  44.9 0.8 %place.1 = (f32[64,128]{1,0:T(8,128)S(1)}, f32[64,128]{1,0:T(8,128)S(1)}) custom-call(s32[1]{0:T(128)} %bitcast.own_ref, s32[16,16]{1,0:T(8,128)S(1)} %copy-done, f32[16,64,128]{2,1,0:T(8,128)S(1)} %all_to_all.10.sums_ref), custom_call_target="tpu_custom_call" | custom-call | tf_op jit(solution)/shard_map/place/pallas_call | solution.py:277
  45.7 1.9 %collective-permute-start.2 = (f32[64,128]{1,0:T(8,128)S(1)}, f32[64,128]{1,0:T(8,128)S(1)}, u32[]{:S(2)}, u32[]{:S(2)}) collective-permute-start(f32[64,128]{1,0:T(8,128)S(1)} %get-tuple-element.18), channel_id=1, source_target_pairs={{0,1},{1,2},{2,3},{3,4},{4,5},{5,6},{6,7},{7,8},{8,9},{9,10},{10,1... | collective-permute-start | bytes 98312 | tf_op jit(solution)/shard_map/ppermute | solution.py:286
  47.6 4.5 %collective-permute-done.2 = f32[64,128]{1,0:T(8,128)S(1)} collective-permute-done((f32[64,128]{1,0:T(8,128)S(1)}, f32[64,128]{1,0:T(8,128)S(1)}, u32[]{:S(2)}, u32[]{:S(2)}) %collective-permute-start.2) | collective-permute-done | bytes 32800 | tf_op jit(solution)/shard_map/ppermute | solution.py:286
  52.1 0.6 %add.3 = f32[64,128]{1,0:T(8,128)} add(f32[64,128]{1,0:T(8,128)S(1)} %get-tuple-element.17, f32[64,128]{1,0:T(8,128)S(1)} %collective-permute-done.2) | non-fusion elementwise | flops 8192 | bytes 98304 | tf_op jit(solution)/shard_map/add | solution.py:287
Async XLA Ops:
  1.8 14.9 %collective-permute-start = (f32[5,4,512]{2,1,0:T(4,128)S(1)}, f32[5,4,512]{2,1,0:T(4,128)S(1)}, u32[]{:S(2)}, u32[]{:S(2)}) collective-permute-start(f32[5,4,512]{2,1,0:T(4,128)S(1)} %get-tuple-element.13), channel_id=1, source_target_pairs={{0,1},{1,2},{2,3},{3,4},{4,5},{5,6},{6,7},{7,8},{8,9},{9,10},{10,1... | collective-permute-start | bytes 122888 | tf_op jit(solution)/shard_map/ppermute | solution.py:239
  3.8 15.1 %all-to-all-start = ((f32[16,2,128]{2,1,0:T(2,128)}), f32[16,2,128]{2,1,0:T(2,128)S(1)}, u32[]{:S(2)}, u32[]{:S(2)}) async-start(f32[16,2,128]{2,1,0:T(2,128)} %get-tuple-element.12), calls=%async_computation | async-start | bytes 32768 | tf_op jit(solution)/shard_map/all_to_all | solution.py:238
  10.8 5.9 %collective-permute-start.1 = (f32[5,1,512]{2,1,0:T(1,128)S(1)}, f32[5,1,512]{2,1,0:T(1,128)S(1)}, u32[]{:S(2)}, u32[]{:S(2)}) collective-permute-start(f32[5,1,512]{2,1,0:T(1,128)S(1)} %get-tuple-element.14), channel_id=1, source_target_pairs={{1,0},{2,1},{3,2},{4,3},{5,4},{6,5},{7,6},{8,7},{9,8},{10,9},{11,1... | collective-permute-start | bytes 30728 | tf_op jit(solution)/shard_map/ppermute | solution.py:240
  18.9 26.0 %copy-start = (s32[16,16]{1,0:T(8,128)S(1)}, s32[16,16]{1,0:T(8,128)}, u32[]{:S(2)}) copy-start(s32[16,16]{1,0:T(8,128)} %offset_ref.1) | copy-start | bytes 3076
  45.7 6.4 %collective-permute-start.2 = (f32[64,128]{1,0:T(8,128)S(1)}, f32[64,128]{1,0:T(8,128)S(1)}, u32[]{:S(2)}, u32[]{:S(2)}) collective-permute-start(f32[64,128]{1,0:T(8,128)S(1)} %get-tuple-element.18), channel_id=1, source_target_pairs={{0,1},{1,2},{2,3},{3,4},{4,5},{5,6},{6,7},{7,8},{8,9},{9,10},{10,1... | collective-permute-start | bytes 98312 | tf_op jit(solution)/shard_map/ppermute | solution.py:286

commit v4 on v3

--- a/solution.py
+++ b/solution.py
@@ -21,23 +21,26 @@
 PARTS = 16
 
 
-def prep_kernel(flow_ref, angle_ref, wide_ref, low_ref, high_ref, edges_ref, sem):
+def prep_kernel(flow_ref, angle_ref, wide_ref, low_ref, high_ref, edges_ref, held_ref, spread_ref, sem):
     steps = flow_ref.shape[1]
+    inward = pltpu.make_async_copy(angle_ref, held_ref, sem.at[2])
+    inward.start()
     copies = [
         pltpu.make_async_copy(flow_ref.at[:, pl.ds(start, ROWS), :], edges_ref.at[side], sem.at[side])
         for side, start in enumerate((steps - ROWS, 0))
     ]
-    copies += [
-        pltpu.make_async_copy(angle_ref, wide_ref.at[group], sem.at[2 + group]) for group in range(wide_ref.shape[0])
-    ]
     for copy in copies:
         copy.start()
-    for copy in copies[:2]:
+    inward.wait()
+    for group in range(spread_ref.shape[0]):
+        spread_ref[group] = held_ref[...]
+    outward = pltpu.make_async_copy(spread_ref, wide_ref, sem.at[3])
+    outward.start()
+    for copy in copies:
         copy.wait()
     low_ref[...] = edges_ref[0, :, ROWS - LAGS :, :]
     high_ref[...] = edges_ref[1, :, :1, :]
-    for copy in copies[2:]:
-        copy.wait()
+    outward.wait()
 
 
 def terms_kernel(edge_ref, own_ref, flow_ref, low_ref, high_ref, area_ref, point_ref, terms_ref, spread_ref, field_ref, part_ref):
@@ -164,7 +167,7 @@
             result = mine[3 * steps :]
             for i in range(3):
                 result = result + place[i] * mine[i * steps : (i + 1) * steps]
-            sums_ref[turn * pair + j] = SCALE * result
+            sums_ref[turn * pair + j] = (SCALE * result).astype(sums_ref.dtype)
 
     for part in range(PARTS):
         fill_weights(places_of(0), spread_ref, even_ref, part)
@@ -198,7 +201,7 @@
     canvas_ref[...] = jnp.zeros_like(canvas_ref)
     for block in range(groups):
         span = pl.ds(offset_ref[own_ref[0], block], steps)
-        canvas_ref[span, :] = canvas_ref[span, :] + sums_ref[block]
+        canvas_ref[span, :] = canvas_ref[span, :] + sums_ref[block].astype(jnp.float32)
     out_ref[...] = canvas_ref[:steps]
     later_ref[...] = canvas_ref[steps : 2 * steps]
 
@@ -231,7 +234,12 @@
         ),
         in_specs=[HBM, HBM],
         out_specs=(HBM, VMEM, VMEM),
-        scratch_shapes=[pltpu.VMEM((2, 5, ROWS, width), jnp.float32), pltpu.SemaphoreType.DMA((2 + groups,))],
+        scratch_shapes=[
+            pltpu.VMEM((2, 5, ROWS, width), jnp.float32),
+            pltpu.VMEM((2, lanes), jnp.float32),
+            pltpu.VMEM((groups, 2, lanes), jnp.float32),
+            pltpu.SemaphoreType.DMA((4,)),
+        ],
         compiler_params=pltpu.CompilerParams(vmem_limit_bytes=8 << 20),
         name="prep",
     )(in_hbm(flow), in_hbm(observer_angles))
@@ -259,7 +267,7 @@
     pair = 2
     sums = pl.pallas_call(
         pair_kernel,
-        out_shape=pltpu.VMEM((groups, steps, lanes), jnp.float32),
+        out_shape=pltpu.VMEM((groups, steps, lanes), jnp.bfloat16),
         in_specs=[VMEM] * 3,
         out_specs=VMEM,
         scratch_shapes=[

time: 53.1 us -> 49.5 us (0.932)
  blocking collectives: 19.2 us -> 16.1 us
  Pallas kernels: 11.6 us -> 11 us
    all_to_all x1, blocking collectives: 19.2 us -> 16.1 us  [local(): sums = lax.all_to_all(sums, 'obs', 0, 0, tiled=True)]
where the time goes in v4:
time: 49.5 us; the launch traced here: 49.2 us
  blocking collectives  16.1 us (33%)
  starting transfers between devices  15.5 us (31%)
  Pallas kernels  11 us (22%)
  waiting for transfers between devices  5.88 us (12%)
  other arithmetic  0.62 us (1%)
    all_to_all x1, blocking collectives, local(): sums = lax.all_to_all(sums, 'obs', 0, 0, tiled=True)  16.1 us
    all_to_all x1, starting transfers between devices, local(): angles = lax.all_to_all(wide, 'obs', 0, 0, tiled=True)  7.05 us
    pallas_call x1, Pallas kernels, local(): pl.pallas_call(pair_kernel, out_shape=pltpu.VMEM((groups, steps, lanes),...  6.82 us
    ppermute x1, starting transfers between devices, local(): high = lax.ppermute(high, 'tm', [(i + 1, i) for i in range(times - 1)])  4.57 us
    ppermute x1, waiting for transfers between devices, local(): carried = lax.ppermute(later, 'tm', [(i, i + 1) for i in range(times - 1)])  4.52 us
    pallas_call x1, Pallas kernels, local(): pl.pallas_call(terms_kernel, out_shape=(pltpu.VMEM((depth // LANES, COMPS...  2.08 us
    ppermute x1, starting transfers between devices, local(): low = lax.ppermute(low, 'tm', [(i, i + 1) for i in range(times - 1)])  1.92 us
    ppermute x1, starting transfers between devices, local(): carried = lax.ppermute(later, 'tm', [(i, i + 1) for i in range(times - 1)])  1.92 us
  transfers between devices with their start and end apart: 4, of which 2 were waited for; matrix products, arithmetic and copies ran while one was open for 0% of the time, Pallas kernels for 4%

profile of v4, /device:TPU:128, one launch (start us, length us, event | category | flops | bytes accessed | tf_op | source)
XLA Modules:
  0.0 49.2 jit_solution(16065276964462184242)
XLA Ops:
  0.0 1.3 %prep.1 = (f32[16,2,128]{2,1,0:T(2,128)}, f32[5,4,512]{2,1,0:T(4,128)S(1)}, f32[5,1,512]{2,1,0:T(1,128)S(1)}) custom-call(f32[5,64,512]{2,1,0:T(8,128)} %flow_ref.3, f32[2,128]{1,0:T(2,128)} %angle_ref.1), custom_call_target="tpu_custom_call" | custom-call | tf_op jit(solution)/shard_map/prep/pallas_call | solution.py:228
  1.3 1.9 %collective-permute-start = (f32[5,4,512]{2,1,0:T(4,128)S(1)}, f32[5,4,512]{2,1,0:T(4,128)S(1)}, u32[]{:S(2)}, u32[]{:S(2)}) collective-permute-start(f32[5,4,512]{2,1,0:T(4,128)S(1)} %get-tuple-element.13), channel_id=1, source_target_pairs={{0,1},{1,2},{2,3},{3,4},{4,5},{5,6},{6,7},{7,8},{8,9},{9,10},{10,1... | collective-permute-start | bytes 122888 | tf_op jit(solution)/shard_map/ppermute | solution.py:247
  3.3 7.0 %all-to-all-start = ((f32[16,2,128]{2,1,0:T(2,128)}), f32[16,2,128]{2,1,0:T(2,128)S(1)}, u32[]{:S(2)}, u32[]{:S(2)}) async-start(f32[16,2,128]{2,1,0:T(2,128)} %get-tuple-element.12), calls=%async_computation | async-start | bytes 32768 | tf_op jit(solution)/shard_map/all_to_all | solution.py:246
  10.3 4.6 %collective-permute-start.1 = (f32[5,1,512]{2,1,0:T(1,128)S(1)}, f32[5,1,512]{2,1,0:T(1,128)S(1)}, u32[]{:S(2)}, u32[]{:S(2)}) collective-permute-start(f32[5,1,512]{2,1,0:T(1,128)S(1)} %get-tuple-element.14), channel_id=1, source_target_pairs={{1,0},{2,1},{3,2},{4,3},{5,4},{6,5},{7,6},{8,7},{9,8},{10,9},{11,1... | collective-permute-start | bytes 30728 | tf_op jit(solution)/shard_map/ppermute | solution.py:248
  14.9 1.4 %collective-permute-done.1.high_ref = f32[5,1,512]{2,1,0:T(1,128)S(1)} collective-permute-done((f32[5,1,512]{2,1,0:T(1,128)S(1)}, f32[5,1,512]{2,1,0:T(1,128)S(1)}, u32[]{:S(2)}, u32[]{:S(2)}) %collective-permute-start.1) | collective-permute-done | bytes 10272 | tf_op jit(solution)/shard_map/ppermute | solution.py:248
  16.3 0.0 collective-permute-done.low_ref
  16.3 2.1 %terms.1 = (bf16[32,256,128]{2,1,0:T(8,128)(2,1)S(1)}, f32[4,512,128]{2,1,0:T(8,128)S(1)}) custom-call(s32[1]{0:T(128)} %bitcast.1.edge_ref, s32[1]{0:T(128)} %bitcast.own_ref, f32[5,64,512]{2,1,0:T(8,128)} %flow_ref.3, f32[5,4,512]{2,1,0:T(4,128)S(1)} %collective-permute-done.low_ref, f32[5,1,512]{2,1,0:T(1,128)S(1)} %collective-permute-done.1.high_ref, ...), custom_call_target="tpu_custom_call" | custom-call | tf_op jit(solution)/shard_map/terms/pallas_call | solution.py:252
  18.3 0.0 copy-start
  18.4 0.0 all-to-all-done.angle_ref
  18.4 6.8 %pairs.1 = bf16[16,64,128]{2,1,0:T(8,128)(2,1)S(1)} custom-call(f32[16,2,128]{2,1,0:T(2,128)S(1)} %all-to-all-done.angle_ref, bf16[32,256,128]{2,1,0:T(8,128)(2,1)S(1)} %get-tuple-element.15.terms_ref, f32[4,512,128]{2,1,0:T(8,128)S(1)} %get-tuple-element.16.spread_ref), custom_call_target="tpu_custom_call" | custom-call | tf_op jit(solution)/shard_map/pairs/pallas_call | solution.py:268
  25.2 16.1 %all_to_all.10.sums_ref = bf16[16,64,128]{2,1,0:T(8,128)(2,1)S(1)} all-to-all(bf16[16,64,128]{2,1,0:T(8,128)(2,1)S(1)} %pairs.1), channel_id=1, replica_groups=mesh['obs'=16,'tm'=32] {'obs'}, dimensions={0} | all-to-all | bytes 524288 | tf_op jit(solution)/shard_map/all_to_all | solution.py:284
  41.3 0.0 copy-done
  41.3 0.8 %place.1 = (f32[64,128]{1,0:T(8,128)S(1)}, f32[64,128]{1,0:T(8,128)S(1)}) custom-call(s32[1]{0:T(128)} %bitcast.own_ref, s32[16,16]{1,0:T(8,128)S(1)} %copy-done, bf16[16,64,128]{2,1,0:T(8,128)(2,1)S(1)} %all_to_all.10.sums_ref), custom_call_target="tpu_custom_call" | custom-call | tf_op jit(solution)/shard_map/place/pallas_call | solution.py:285
  42.1 1.9 %collective-permute-start.2 = (f32[64,128]{1,0:T(8,128)S(1)}, f32[64,128]{1,0:T(8,128)S(1)}, u32[]{:S(2)}, u32[]{:S(2)}) collective-permute-start(f32[64,128]{1,0:T(8,128)S(1)} %get-tuple-element.18), channel_id=1, source_target_pairs={{0,1},{1,2},{2,3},{3,4},{4,5},{5,6},{6,7},{7,8},{8,9},{9,10},{10,1... | collective-permute-start | bytes 98312 | tf_op jit(solution)/shard_map/ppermute | solution.py:294
  44.1 4.5 %collective-permute-done.2 = f32[64,128]{1,0:T(8,128)S(1)} collective-permute-done((f32[64,128]{1,0:T(8,128)S(1)}, f32[64,128]{1,0:T(8,128)S(1)}, u32[]{:S(2)}, u32[]{:S(2)}) %collective-permute-start.2) | collective-permute-done | bytes 32800 | tf_op jit(solution)/shard_map/ppermute | solution.py:294
  48.6 0.6 %add.3 = f32[64,128]{1,0:T(8,128)} add(f32[64,128]{1,0:T(8,128)S(1)} %get-tuple-element.17, f32[64,128]{1,0:T(8,128)S(1)} %collective-permute-done.2) | non-fusion elementwise | flops 8192 | bytes 98304 | tf_op jit(solution)/shard_map/add | solution.py:295
Async XLA Ops:
  1.3 14.9 %collective-permute-start = (f32[5,4,512]{2,1,0:T(4,128)S(1)}, f32[5,4,512]{2,1,0:T(4,128)S(1)}, u32[]{:S(2)}, u32[]{:S(2)}) collective-permute-start(f32[5,4,512]{2,1,0:T(4,128)S(1)} %get-tuple-element.13), channel_id=1, source_target_pairs={{0,1},{1,2},{2,3},{3,4},{4,5},{5,6},{6,7},{7,8},{8,9},{9,10},{10,1... | collective-permute-start | bytes 122888 | tf_op jit(solution)/shard_map/ppermute | solution.py:247
  3.3 15.1 %all-to-all-start = ((f32[16,2,128]{2,1,0:T(2,128)}), f32[16,2,128]{2,1,0:T(2,128)S(1)}, u32[]{:S(2)}, u32[]{:S(2)}) async-start(f32[16,2,128]{2,1,0:T(2,128)} %get-tuple-element.12), calls=%async_computation | async-start | bytes 32768 | tf_op jit(solution)/shard_map/all_to_all | solution.py:246
  10.3 5.9 %collective-permute-start.1 = (f32[5,1,512]{2,1,0:T(1,128)S(1)}, f32[5,1,512]{2,1,0:T(1,128)S(1)}, u32[]{:S(2)}, u32[]{:S(2)}) collective-permute-start(f32[5,1,512]{2,1,0:T(1,128)S(1)} %get-tuple-element.14), channel_id=1, source_target_pairs={{1,0},{2,1},{3,2},{4,3},{5,4},{6,5},{7,6},{8,7},{9,8},{10,9},{11,1... | collective-permute-start | bytes 30728 | tf_op jit(solution)/shard_map/ppermute | solution.py:248
  18.3 23.0 %copy-start = (s32[16,16]{1,0:T(8,128)S(1)}, s32[16,16]{1,0:T(8,128)}, u32[]{:S(2)}) copy-start(s32[16,16]{1,0:T(8,128)} %offset_ref.1) | copy-start | bytes 3076
  42.1 6.4 %collective-permute-start.2 = (f32[64,128]{1,0:T(8,128)S(1)}, f32[64,128]{1,0:T(8,128)S(1)}, u32[]{:S(2)}, u32[]{:S(2)}) collective-permute-start(f32[64,128]{1,0:T(8,128)S(1)} %get-tuple-element.18), channel_id=1, source_target_pairs={{0,1},{1,2},{2,3},{3,4},{4,5},{5,6},{6,7},{7,8},{8,9},{9,10},{10,1... | collective-permute-start | bytes 98312 | tf_op jit(solution)/shard_map/ppermute | solution.py:294

commit v5 on v4

--- a/solution.py
+++ b/solution.py
@@ -21,7 +21,7 @@
 PARTS = 16
 
 
-def prep_kernel(flow_ref, angle_ref, wide_ref, low_ref, high_ref, edges_ref, held_ref, spread_ref, sem):
+def prep_kernel(time_ref, flow_ref, angle_ref, wide_ref, core_ref, chip_ref, edges_ref, held_ref, spread_ref, sem):
     steps = flow_ref.shape[1]
     inward = pltpu.make_async_copy(angle_ref, held_ref, sem.at[2])
     inward.start()
@@ -38,15 +38,21 @@
     outward.start()
     for copy in copies:
         copy.wait()
-    low_ref[...] = edges_ref[0, :, ROWS - LAGS :, :]
-    high_ref[...] = edges_ref[1, :, :1, :]
+    even = time_ref[0] % 2 == 0
+    last = edges_ref[0, :, ROWS - LAGS :, :]
+    first = edges_ref[1, :, :LAGS, :]
+    core_ref[...] = jnp.where(even, last, first)
+    chip_ref[...] = jnp.where(even, first, last)
     outward.wait()
 
 
-def terms_kernel(edge_ref, own_ref, flow_ref, low_ref, high_ref, area_ref, point_ref, terms_ref, spread_ref, field_ref, part_ref):
+def terms_kernel(time_ref, own_ref, flow_ref, core_ref, chip_ref, area_ref, point_ref, terms_ref, spread_ref, field_ref, part_ref):
     steps = flow_ref.shape[1]
     width = flow_ref.shape[2]
     count = steps + ROWS
+    even = time_ref[0] % 2 == 0
+    low = jnp.where(even, chip_ref[...], core_ref[...])
+    high = jnp.where(even, core_ref[:, :1, :], chip_ref[:, :1, :])
     for cut in range(width // LANES):
         lanes = slice(cut * LANES, (cut + 1) * LANES)
         area = [area_ref[i : i + 1, lanes] for i in range(3)]
@@ -63,12 +69,12 @@
                 field_ref[1 + i, cut, start : start + rows, :] = pressure * area[i] + mass_flux * velocity[i]
 
         field_ref[:, cut, ROWS + steps :, :] = jnp.zeros((4, ROWS, LANES), jnp.float32)
-        fields(low_ref, ROWS - LAGS, LAGS)
+        fields(low, ROWS - LAGS, LAGS)
         fields(flow_ref, ROWS, steps)
-        fields(high_ref, ROWS + steps, 1)
+        fields(high, ROWS + steps, 1)
         first = ROWS - LAGS + 1
         row = lax.broadcasted_iota(jnp.int32, (count, LANES), 0)
-        keep = jnp.where(jnp.logical_or(row >= LAGS - 1, edge_ref[0] != 0), 1.0, 0.0)
+        keep = jnp.where(jnp.logical_or(row >= LAGS - 1, time_ref[0] != 0), 1.0, 0.0)
         rates = [
             (0.5 * keep)
             * (field_ref[k, cut, first + 1 : first + 1 + count, :] - field_ref[k, cut, first - 1 : first - 1 + count, :])
@@ -225,14 +231,15 @@
     groups = lax.axis_size("obs")
     lanes = observer_angles.shape[1]
     times = lax.axis_size("tm")
-    wide, low, high = pl.pallas_call(
+    time = lax.axis_index("tm").astype(jnp.int32).reshape(1)
+    wide, to_core, to_chip = pl.pallas_call(
         prep_kernel,
         out_shape=(
             jax.ShapeDtypeStruct((groups, 2, lanes), jnp.float32),
             pltpu.VMEM((5, LAGS, width), jnp.float32),
-            pltpu.VMEM((5, 1, width), jnp.float32),
+            pltpu.VMEM((5, LAGS, width), jnp.float32),
         ),
-        in_specs=[HBM, HBM],
+        in_specs=[SMEM, HBM, HBM],
         out_specs=(HBM, VMEM, VMEM),
         scratch_shapes=[
             pltpu.VMEM((2, 5, ROWS, width), jnp.float32),
@@ -242,11 +249,11 @@
         ],
         compiler_params=pltpu.CompilerParams(vmem_limit_bytes=8 << 20),
         name="prep",
-    )(in_hbm(flow), in_hbm(observer_angles))
+    )(time, in_hbm(flow), in_hbm(observer_angles))
     angles = lax.all_to_all(wide, "obs", 0, 0, tiled=True)
-    low = lax.ppermute(low, "tm", [(i, i + 1) for i in range(times - 1)])
-    high = lax.ppermute(high, "tm", [(i + 1, i) for i in range(times - 1)])
-    edge = lax.axis_index("tm").astype(jnp.int32).reshape(1)
+    from_core = lax.ppermute(to_core, "tm", [(i, i ^ 1) for i in range(times)])
+    swaps = [(i, i + 1) for i in range(1, times - 1, 2)]
+    from_chip = lax.ppermute(to_chip, "tm", swaps + [(j, i) for i, j in swaps])
     own = lax.axis_index("obs").astype(jnp.int32).reshape(1)
     depth = 2 * LAGS * width
     terms, spread = pl.pallas_call(
@@ -263,7 +270,7 @@
         ],
         compiler_params=pltpu.CompilerParams(vmem_limit_bytes=16 << 20),
         name="terms",
-    )(edge, own, in_hbm(flow), near_core(low), near_core(high), in_hbm(area_vec), in_hbm(point_pos))
+    )(time, own, in_hbm(flow), near_core(from_core), near_core(from_chip), in_hbm(area_vec), in_hbm(point_pos))
     pair = 2
     sums = pl.pallas_call(
         pair_kernel,

time: 49.5 us -> 48.6 us (0.982)
  the two profiles are of different devices: /device:TPU:128 before, /device:TPU:384 now
where the time goes in v5:
time: 48.6 us; the launch traced here: 48.3 us
  starting transfers between devices  15.1 us (31%)
  blocking collectives  11.5 us (24%)
  Pallas kernels  11 us (23%)
  waiting for transfers between devices  10 us (21%)
  other arithmetic  0.62 us (1%)
    all_to_all x1, blocking collectives, local(): sums = lax.all_to_all(sums, 'obs', 0, 0, tiled=True)  11.5 us
    all_to_all x1, starting transfers between devices, local(): angles = lax.all_to_all(wide, 'obs', 0, 0, tiled=True)  7.05 us
    pallas_call x1, Pallas kernels, local(): pl.pallas_call(pair_kernel, out_shape=pltpu.VMEM((groups, steps, lanes),...  6.81 us
    all_to_all x1, waiting for transfers between devices, local(): angles = lax.all_to_all(wide, 'obs', 0, 0, tiled=True)  5.51 us
    ppermute x1, waiting for transfers between devices, local(): carried = lax.ppermute(later, 'tm', [(i, i + 1) for i in range(times - 1)])  4.52 us
    ppermute x1, starting transfers between devices, local(): from_chip = lax.ppermute(to_chip, 'tm', swaps + [(j, i) for i, j in swaps])  4.23 us
    pallas_call x1, Pallas kernels, local(): pl.pallas_call(terms_kernel, out_shape=(pltpu.VMEM((depth // LANES, COMPS...  2.05 us
    ppermute x1, starting transfers between devices, local(): from_core = lax.ppermute(to_core, 'tm', [(i, i ^ 1) for i in range(times)])  1.92 us
  transfers between devices with their start and end apart: 4, of which 2 were waited for; matrix products, arithmetic and copies ran while one was open for 0% of the time, Pallas kernels for 4%

profile of v5, /device:TPU:384, one launch (start us, length us, event | category | flops | bytes accessed | tf_op | source)
XLA Modules:
  0.0 48.3 jit_solution(16957568367957498776)
XLA Ops:
  0.0 1.3 %prep.1 = (f32[16,2,128]{2,1,0:T(2,128)}, f32[5,4,512]{2,1,0:T(4,128)S(1)}, f32[5,4,512]{2,1,0:T(4,128)S(1)}) custom-call(s32[1]{0:T(128)} %bitcast.1.time_ref, f32[5,64,512]{2,1,0:T(8,128)} %flow_ref.3, f32[2,128]{1,0:T(2,128)} %angle_ref.1), custom_call_target="tpu_custom_call" | custom-call | tf_op jit(solution)/shard_map/prep/pallas_call | solution.py:235
  1.3 1.9 %collective-permute-start = (f32[5,4,512]{2,1,0:T(4,128)S(1)}, f32[5,4,512]{2,1,0:T(4,128)S(1)}, u32[]{:S(2)}, u32[]{:S(2)}) collective-permute-start(f32[5,4,512]{2,1,0:T(4,128)S(1)} %get-tuple-element.13), channel_id=1, source_target_pairs={{0,1},{1,0},{2,3},{3,2},{4,5},{5,4},{6,7},{7,6},{8,9},{9,8},{10,11... | collective-permute-start | bytes 122888 | tf_op jit(solution)/shard_map/ppermute | solution.py:254
  3.3 4.2 %collective-permute-start.1 = (f32[5,4,512]{2,1,0:T(4,128)S(1)}, f32[5,4,512]{2,1,0:T(4,128)S(1)}, u32[]{:S(2)}, u32[]{:S(2)}) collective-permute-start(f32[5,4,512]{2,1,0:T(4,128)S(1)} %get-tuple-element.14), channel_id=1, source_target_pairs={{1,2},{3,4},{5,6},{7,8},{9,10},{11,12},{13,14},{15,16},{17,18},{19... | collective-permute-start | bytes 122888 | tf_op jit(solution)/shard_map/ppermute | solution.py:256
  7.5 7.0 %all-to-all-start = ((f32[16,2,128]{2,1,0:T(2,128)}), f32[16,2,128]{2,1,0:T(2,128)S(1)}, u32[]{:S(2)}, u32[]{:S(2)}) async-start(f32[16,2,128]{2,1,0:T(2,128)} %get-tuple-element.12), calls=%async_computation | async-start | bytes 32768 | tf_op jit(solution)/shard_map/all_to_all | solution.py:253
  14.6 0.0 collective-permute-done.core_ref
  14.6 0.0 collective-permute-done.1.chip_ref
  14.6 2.1 %terms.1 = (bf16[32,256,128]{2,1,0:T(8,128)(2,1)S(1)}, f32[4,512,128]{2,1,0:T(8,128)S(1)}) custom-call(s32[1]{0:T(128)} %bitcast.1.time_ref, s32[1]{0:T(128)} %bitcast.own_ref, f32[5,64,512]{2,1,0:T(8,128)} %flow_ref.3, f32[5,4,512]{2,1,0:T(4,128)S(1)} %collective-permute-done.core_ref, f32[5,4,512]{2,1,0:T(4,128)S(1)} %collective-permute-done.1.chip_ref, ...), custom_call_target="tpu_custom_call" | custom-call | tf_op jit(solution)/shard_map/terms/pallas_call | solution.py:259
  16.6 0.0 copy-start
  16.6 5.5 %all-to-all-done.angle_ref = f32[16,2,128]{2,1,0:T(2,128)S(1)} async-done(((f32[16,2,128]{2,1,0:T(2,128)}), f32[16,2,128]{2,1,0:T(2,128)S(1)}, u32[]{:S(2)}, u32[]{:S(2)}) %all-to-all-start) | async-done | bytes 16416 | tf_op jit(solution)/shard_map/all_to_all | solution.py:253
  22.1 6.8 %pairs.1 = bf16[16,64,128]{2,1,0:T(8,128)(2,1)S(1)} custom-call(f32[16,2,128]{2,1,0:T(2,128)S(1)} %all-to-all-done.angle_ref, bf16[32,256,128]{2,1,0:T(8,128)(2,1)S(1)} %get-tuple-element.15.terms_ref, f32[4,512,128]{2,1,0:T(8,128)S(1)} %get-tuple-element.16.spread_ref), custom_call_target="tpu_custom_call" | custom-call | tf_op jit(solution)/shard_map/pairs/pallas_call | solution.py:275
  29.0 11.5 %all_to_all.10.sums_ref = bf16[16,64,128]{2,1,0:T(8,128)(2,1)S(1)} all-to-all(bf16[16,64,128]{2,1,0:T(8,128)(2,1)S(1)} %pairs.1), channel_id=1, replica_groups=mesh['obs'=16,'tm'=32] {'obs'}, dimensions={0} | all-to-all | bytes 524288 | tf_op jit(solution)/shard_map/all_to_all | solution.py:291
  40.5 0.0 copy-done
  40.5 0.8 %place.1 = (f32[64,128]{1,0:T(8,128)S(1)}, f32[64,128]{1,0:T(8,128)S(1)}) custom-call(s32[1]{0:T(128)} %bitcast.own_ref, s32[16,16]{1,0:T(8,128)S(1)} %copy-done, bf16[16,64,128]{2,1,0:T(8,128)(2,1)S(1)} %all_to_all.10.sums_ref), custom_call_target="tpu_custom_call" | custom-call | tf_op jit(solution)/shard_map/place/pallas_call | solution.py:292
  41.3 1.9 %collective-permute-start.2 = (f32[64,128]{1,0:T(8,128)S(1)}, f32[64,128]{1,0:T(8,128)S(1)}, u32[]{:S(2)}, u32[]{:S(2)}) collective-permute-start(f32[64,128]{1,0:T(8,128)S(1)} %get-tuple-element.18), channel_id=1, source_target_pairs={{0,1},{1,2},{2,3},{3,4},{4,5},{5,6},{6,7},{7,8},{8,9},{9,10},{10,1... | collective-permute-start | bytes 98312 | tf_op jit(solution)/shard_map/ppermute | solution.py:301
  43.2 4.5 %collective-permute-done.2 = f32[64,128]{1,0:T(8,128)S(1)} collective-permute-done((f32[64,128]{1,0:T(8,128)S(1)}, f32[64,128]{1,0:T(8,128)S(1)}, u32[]{:S(2)}, u32[]{:S(2)}) %collective-permute-start.2) | collective-permute-done | bytes 32800 | tf_op jit(solution)/shard_map/ppermute | solution.py:301
  47.7 0.6 %add.3 = f32[64,128]{1,0:T(8,128)} add(f32[64,128]{1,0:T(8,128)S(1)} %get-tuple-element.17, f32[64,128]{1,0:T(8,128)S(1)} %collective-permute-done.2) | non-fusion elementwise | flops 8192 | bytes 98304 | tf_op jit(solution)/shard_map/add | solution.py:302
Async XLA Ops:
  1.3 13.2 %collective-permute-start = (f32[5,4,512]{2,1,0:T(4,128)S(1)}, f32[5,4,512]{2,1,0:T(4,128)S(1)}, u32[]{:S(2)}, u32[]{:S(2)}) collective-permute-start(f32[5,4,512]{2,1,0:T(4,128)S(1)} %get-tuple-element.13), channel_id=1, source_target_pairs={{0,1},{1,0},{2,3},{3,2},{4,5},{5,4},{6,7},{7,6},{8,9},{9,8},{10,11... | collective-permute-start | bytes 122888 | tf_op jit(solution)/shard_map/ppermute | solution.py:254
  3.3 11.3 %collective-permute-start.1 = (f32[5,4,512]{2,1,0:T(4,128)S(1)}, f32[5,4,512]{2,1,0:T(4,128)S(1)}, u32[]{:S(2)}, u32[]{:S(2)}) collective-permute-start(f32[5,4,512]{2,1,0:T(4,128)S(1)} %get-tuple-element.14), channel_id=1, source_target_pairs={{1,2},{3,4},{5,6},{7,8},{9,10},{11,12},{13,14},{15,16},{17,18},{19... | collective-permute-start | bytes 122888 | tf_op jit(solution)/shard_map/ppermute | solution.py:256
  7.5 14.7 %all-to-all-start = ((f32[16,2,128]{2,1,0:T(2,128)}), f32[16,2,128]{2,1,0:T(2,128)S(1)}, u32[]{:S(2)}, u32[]{:S(2)}) async-start(f32[16,2,128]{2,1,0:T(2,128)} %get-tuple-element.12), calls=%async_computation | async-start | bytes 32768 | tf_op jit(solution)/shard_map/all_to_all | solution.py:253
  16.6 23.8 %copy-start = (s32[16,16]{1,0:T(8,128)S(1)}, s32[16,16]{1,0:T(8,128)}, u32[]{:S(2)}) copy-start(s32[16,16]{1,0:T(8,128)} %offset_ref.1) | copy-start | bytes 3076
  41.3 6.4 %collective-permute-start.2 = (f32[64,128]{1,0:T(8,128)S(1)}, f32[64,128]{1,0:T(8,128)S(1)}, u32[]{:S(2)}, u32[]{:S(2)}) collective-permute-start(f32[64,128]{1,0:T(8,128)S(1)} %get-tuple-element.18), channel_id=1, source_target_pairs={{0,1},{1,2},{2,3},{3,4},{4,5},{5,6},{6,7},{7,8},{8,9},{9,10},{10,1... | collective-permute-start | bytes 98312 | tf_op jit(solution)/shard_map/ppermute | solution.py:301

commit v6 on v5

--- a/solution.py
+++ b/solution.py
@@ -46,9 +46,35 @@
     outward.wait()
 
 
-def terms_kernel(time_ref, own_ref, flow_ref, core_ref, chip_ref, area_ref, point_ref, terms_ref, spread_ref, field_ref, part_ref):
-    steps = flow_ref.shape[1]
+def fluxes(flow, area):
+    density = 1.0 + 0.2 * flow[0]
+    velocity = [0.4 * flow[1 + i] for i in range(3)]
+    normal_flux = velocity[0] * area[0] + velocity[1] * area[1] + velocity[2] * area[2]
+    mass_flux = density * normal_flux
+    return [mass_flux] + [flow[4] * area[i] + mass_flux * velocity[i] for i in range(3)]
+
+
+def early_kernel(own_ref, offset_ref, flow_ref, area_ref, point_ref, field_ref, spread_ref, own_area_ref, own_point_ref, delay_ref):
     width = flow_ref.shape[2]
+    for block in range(delay_ref.shape[0]):
+        delay_ref[block] = offset_ref[own_ref[0], block]
+    own_area_ref[...] = area_ref[...]
+    own_point_ref[...] = point_ref[...]
+    point = [(1.0 / SOUND_STEP) * point_ref[i : i + 1, :] for i in range(3)]
+    reach = RADIUS * RADIUS + point[0] * point[0] + point[1] * point[1] + point[2] * point[2]
+    turned = jnp.transpose(jnp.concatenate([2.0 * point[0], 2.0 * point[1], 2.0 * point[2], reach] * 2, axis=0))
+    for cut in range(width // LANES):
+        lanes = slice(cut * LANES, (cut + 1) * LANES)
+        area = [area_ref[i : i + 1, lanes] for i in range(3)]
+        for k, field in enumerate(fluxes([flow_ref[i, :, lanes] for i in range(5)], area)):
+            field_ref[k, cut] = field
+        for i in range(4):
+            spread_ref[i, lanes, :] = jnp.broadcast_to(turned[lanes, i : i + 1], (LANES, LANES))
+
+
+def terms_kernel(time_ref, early_ref, core_ref, chip_ref, area_ref, point_ref, terms_ref, field_ref, part_ref):
+    steps = early_ref.shape[2]
+    width = area_ref.shape[1]
     count = steps + ROWS
     even = time_ref[0] % 2 == 0
     low = jnp.where(even, chip_ref[...], core_ref[...])
@@ -57,21 +83,11 @@
         lanes = slice(cut * LANES, (cut + 1) * LANES)
         area = [area_ref[i : i + 1, lanes] for i in range(3)]
         point = [(1.0 / SOUND_STEP) * point_ref[i : i + 1, lanes] for i in range(3)]
-
-        def fields(source, start, rows):
-            density = 1.0 + 0.2 * source[0, :, lanes]
-            velocity = [0.4 * source[1 + i, :, lanes] for i in range(3)]
-            pressure = source[4, :, lanes]
-            normal_flux = velocity[0] * area[0] + velocity[1] * area[1] + velocity[2] * area[2]
-            mass_flux = density * normal_flux
-            field_ref[0, cut, start : start + rows, :] = mass_flux
-            for i in range(3):
-                field_ref[1 + i, cut, start : start + rows, :] = pressure * area[i] + mass_flux * velocity[i]
-
         field_ref[:, cut, ROWS + steps :, :] = jnp.zeros((4, ROWS, LANES), jnp.float32)
-        fields(low, ROWS - LAGS, LAGS)
-        fields(flow_ref, ROWS, steps)
-        fields(high, ROWS + steps, 1)
+        field_ref[:, cut, ROWS : ROWS + steps, :] = early_ref[:, cut]
+        for halo, start in ((low, ROWS - LAGS), (high, ROWS + steps)):
+            for k, field in enumerate(fluxes(halo[:, :, lanes], area)):
+                field_ref[k, cut, start : start + halo.shape[1], :] = field
         first = ROWS - LAGS + 1
         row = lax.broadcasted_iota(jnp.int32, (count, LANES), 0)
         keep = jnp.where(jnp.logical_or(row >= LAGS - 1, time_ref[0] != 0), 1.0, 0.0)
@@ -97,11 +113,6 @@
                     terms_ref[block, comp * steps : (comp + 1) * steps, :] = part_ref[
                         cut, family * COMPS + comp, start : start + steps, :
                     ].astype(jnp.bfloat16)
-        turned = jnp.transpose(
-            jnp.concatenate([2.0 * point[0], 2.0 * point[1], 2.0 * point[2], reach] * 2, axis=0)
-        )
-        for i in range(4):
-            spread_ref[i, lanes, :] = jnp.broadcast_to(turned[:, i : i + 1], (LANES, LANES))
 
 
 def fill_weights(places, spread_ref, weights_ref, part):
@@ -202,11 +213,11 @@
     finish(turns - 1, rest_ref)
 
 
-def place_kernel(own_ref, offset_ref, sums_ref, out_ref, later_ref, canvas_ref):
+def place_kernel(delay_ref, sums_ref, out_ref, later_ref, canvas_ref):
     groups, steps, _ = sums_ref.shape
     canvas_ref[...] = jnp.zeros_like(canvas_ref)
     for block in range(groups):
-        span = pl.ds(offset_ref[own_ref[0], block], steps)
+        span = pl.ds(delay_ref[block], steps)
         canvas_ref[span, :] = canvas_ref[span, :] + sums_ref[block].astype(jnp.float32)
     out_ref[...] = canvas_ref[:steps]
     later_ref[...] = canvas_ref[steps : 2 * steps]
@@ -256,21 +267,33 @@
     from_chip = lax.ppermute(to_chip, "tm", swaps + [(j, i) for i, j in swaps])
     own = lax.axis_index("obs").astype(jnp.int32).reshape(1)
     depth = 2 * LAGS * width
-    terms, spread = pl.pallas_call(
+    cuts = width // LANES
+    early, spread, own_area, own_point, delays = pl.pallas_call(
+        early_kernel,
+        out_shape=(
+            pltpu.VMEM((4, cuts, steps, LANES), jnp.float32),
+            pltpu.VMEM((4, width, LANES), jnp.float32),
+            pltpu.VMEM(area_vec.shape, jnp.float32),
+            pltpu.VMEM(point_pos.shape, jnp.float32),
+            pltpu.SMEM((groups,), jnp.int32),
+        ),
+        in_specs=[SMEM] * 2 + [VMEM] * 3,
+        out_specs=(VMEM,) * 4 + (SMEM,),
+        compiler_params=pltpu.CompilerParams(vmem_limit_bytes=16 << 20),
+        name="early",
+    )(own, in_hbm(band_offset), in_hbm(flow), in_hbm(area_vec), in_hbm(point_pos))
+    terms = pl.pallas_call(
         terms_kernel,
-        out_shape=(
-            pltpu.VMEM((depth // LANES, COMPS * steps, LANES), jnp.bfloat16),
-            pltpu.VMEM((4, width, LANES), jnp.float32),
-        ),
-        in_specs=[SMEM] * 2 + [VMEM] * 5,
-        out_specs=(VMEM, VMEM),
+        out_shape=pltpu.VMEM((depth // LANES, COMPS * steps, LANES), jnp.bfloat16),
+        in_specs=[SMEM] + [VMEM] * 5,
+        out_specs=VMEM,
         scratch_shapes=[
-            pltpu.VMEM((4, width // LANES, steps + 2 * ROWS, LANES), jnp.float32),
-            pltpu.VMEM((width // LANES, 2 * COMPS, steps + ROWS, LANES), jnp.float32),
+            pltpu.VMEM((4, cuts, steps + 2 * ROWS, LANES), jnp.float32),
+            pltpu.VMEM((cuts, 2 * COMPS, steps + ROWS, LANES), jnp.float32),
         ],
         compiler_params=pltpu.CompilerParams(vmem_limit_bytes=16 << 20),
         name="terms",
-    )(time, own, in_hbm(flow), near_core(from_core), near_core(from_chip), in_hbm(area_vec), in_hbm(point_pos))
+    )(time, *map(near_core, (early, from_core, from_chip, own_area, own_point)))
     pair = 2
     sums = pl.pallas_call(
         pair_kernel,
@@ -292,12 +315,12 @@
     out, later = pl.pallas_call(
         place_kernel,
         out_shape=(pltpu.VMEM((steps, lanes), jnp.float32),) * 2,
-        in_specs=[SMEM, SMEM, VMEM],
+        in_specs=[SMEM, VMEM],
         out_specs=(VMEM, VMEM),
         scratch_shapes=[pltpu.VMEM((2 * steps, lanes), jnp.float32)],
         compiler_params=pltpu.CompilerParams(vmem_limit_bytes=8 << 20),
         name="place",
-    )(own, band_offset, near_core(sums))
+    )(pltpu.with_memory_space_constraint(delays, pltpu.SMEM), near_core(sums))
     carried = lax.ppermute(later, "tm", [(i, i + 1) for i in range(times - 1)])
     return out + carried
 

time: 48.6 us -> 48 us (0.988)
  Pallas kernels: 11 us -> 10.4 us
    pallas_call x1, Pallas kernels: 0.8 us -> 0.13 us  [local(): pl.pallas_call(place_kernel, out_shape=(pltpu.VMEM((steps, lanes), jnp.fl...]
    pallas_call x1 -> x2, Pallas kernels: 2.05 us -> 2.09 us  [the longest x1 1.63 us: local(): pl.pallas_call(early_kernel, out_shape=(pltpu.VMEM((4, cuts, steps, LANES...]
where the time goes in v6:
time: 48 us; the launch traced here: 47.7 us
  starting transfers between devices  15.1 us (31%)
  blocking collectives  11.5 us (24%)
  Pallas kernels  10.4 us (22%)
  waiting for transfers between devices  9.99 us (21%)
  other arithmetic  0.62 us (1%)
    all_to_all x1, blocking collectives, local(): sums = lax.all_to_all(sums, 'obs', 0, 0, tiled=True)  11.5 us
    all_to_all x1, starting transfers between devices, local(): angles = lax.all_to_all(wide, 'obs', 0, 0, tiled=True)  7.05 us
    pallas_call x1, Pallas kernels, local(): pl.pallas_call(pair_kernel, out_shape=pltpu.VMEM((groups, steps, lanes),...  6.81 us
    all_to_all x1, waiting for transfers between devices, local(): angles = lax.all_to_all(wide, 'obs', 0, 0, tiled=True)  5.47 us
    ppermute x1, waiting for transfers between devices, local(): carried = lax.ppermute(later, 'tm', [(i, i + 1) for i in range(times - 1)])  4.52 us
    ppermute x1, starting transfers between devices, local(): from_chip = lax.ppermute(to_chip, 'tm', swaps + [(j, i) for i, j in swaps])  4.23 us
    ppermute x1, starting transfers between devices, local(): from_core = lax.ppermute(to_core, 'tm', [(i, i ^ 1) for i in range(times)])  1.92 us
    ppermute x1, starting transfers between devices, local(): carried = lax.ppermute(later, 'tm', [(i, i + 1) for i in range(times - 1)])  1.92 us
  transfers between devices with their start and end apart: 4, of which 2 were waited for; matrix products, arithmetic and copies ran while one was open for 0% of the time, Pallas kernels for 4%

profile of v6, /device:TPU:384, one launch (start us, length us, event | category | flops | bytes accessed | tf_op | source)
XLA Modules:
  0.0 47.7 jit_solution(16040706821089952886)
XLA Ops:
  0.0 1.3 %prep.1 = (f32[16,2,128]{2,1,0:T(2,128)}, f32[5,4,512]{2,1,0:T(4,128)S(1)}, f32[5,4,512]{2,1,0:T(4,128)S(1)}) custom-call(s32[1]{0:T(128)} %bitcast.1.time_ref, f32[5,64,512]{2,1,0:T(8,128)} %flow_ref.3, f32[2,128]{1,0:T(2,128)} %angle_ref.1), custom_call_target="tpu_custom_call" | custom-call | tf_op jit(solution)/shard_map/prep/pallas_call | solution.py:246
  1.3 1.9 %collective-permute-start = (f32[5,4,512]{2,1,0:T(4,128)S(1)}, f32[5,4,512]{2,1,0:T(4,128)S(1)}, u32[]{:S(2)}, u32[]{:S(2)}) collective-permute-start(f32[5,4,512]{2,1,0:T(4,128)S(1)} %get-tuple-element.18), channel_id=1, source_target_pairs={{0,1},{1,0},{2,3},{3,2},{4,5},{5,4},{6,7},{7,6},{8,9},{9,8},{10,11... | collective-permute-start | bytes 122888 | tf_op jit(solution)/shard_map/ppermute | solution.py:265
  3.3 4.2 %collective-permute-start.1 = (f32[5,4,512]{2,1,0:T(4,128)S(1)}, f32[5,4,512]{2,1,0:T(4,128)S(1)}, u32[]{:S(2)}, u32[]{:S(2)}) collective-permute-start(f32[5,4,512]{2,1,0:T(4,128)S(1)} %get-tuple-element.19), channel_id=1, source_target_pairs={{1,2},{3,4},{5,6},{7,8},{9,10},{11,12},{13,14},{15,16},{17,18},{19... | collective-permute-start | bytes 122888 | tf_op jit(solution)/shard_map/ppermute | solution.py:267
  7.5 7.0 %all-to-all-start = ((f32[16,2,128]{2,1,0:T(2,128)}), f32[16,2,128]{2,1,0:T(2,128)S(1)}, u32[]{:S(2)}, u32[]{:S(2)}) async-start(f32[16,2,128]{2,1,0:T(2,128)} %get-tuple-element.16), calls=%async_computation | async-start | bytes 32768 | tf_op jit(solution)/shard_map/all_to_all | solution.py:264
  14.6 1.6 %early.1 = (f32[4,4,64,128]{3,2,1,0:T(8,128)S(1)}, f32[4,512,128]{2,1,0:T(8,128)S(1)}, f32[3,512]{1,0:T(4,128)S(1)}, f32[3,512]{1,0:T(4,128)S(1)}, s32[16]{0:T(128)S(4)}) custom-call(s32[1]{0:T(128)} %bitcast.own_ref, s32[16,16]{1,0:T(8,128)} %offset_ref.1, f32[5,64,512]{2,1,0:T(8,128)} %flow_ref.3, f32[3,512]{1,0:T(4,128)} %area_ref.1, f32[3,512]{1,0:T(4,128)} %point_ref.1), custom_call_target="tpu_custom_call" | custom-call | tf_op jit(solution)/shard_map/early/pallas_call | solution.py:271
  16.2 0.0 collective-permute-done.core_ref
  16.2 0.0 collective-permute-done.1.chip_ref
  16.2 0.5 terms.1.terms_ref
  16.7 5.5 %all-to-all-done.angle_ref = f32[16,2,128]{2,1,0:T(2,128)S(1)} async-done(((f32[16,2,128]{2,1,0:T(2,128)}), f32[16,2,128]{2,1,0:T(2,128)S(1)}, u32[]{:S(2)}, u32[]{:S(2)}) %all-to-all-start) | async-done | bytes 16416 | tf_op jit(solution)/shard_map/all_to_all | solution.py:264
  22.1 6.8 %pairs.1 = bf16[16,64,128]{2,1,0:T(8,128)(2,1)S(1)} custom-call(f32[16,2,128]{2,1,0:T(2,128)S(1)} %all-to-all-done.angle_ref, bf16[32,256,128]{2,1,0:T(8,128)(2,1)S(1)} %terms.1.terms_ref, f32[4,512,128]{2,1,0:T(8,128)S(1)} %get-tuple-element.22.spread_ref), custom_call_target="tpu_custom_call" | custom-call | tf_op jit(solution)/shard_map/pairs/pallas_call | solution.py:298
  29.0 11.5 %all_to_all.10.sums_ref = bf16[16,64,128]{2,1,0:T(8,128)(2,1)S(1)} all-to-all(bf16[16,64,128]{2,1,0:T(8,128)(2,1)S(1)} %pairs.1), channel_id=1, replica_groups=mesh['obs'=16,'tm'=32] {'obs'}, dimensions={0} | all-to-all | bytes 524288 | tf_op jit(solution)/shard_map/all_to_all | solution.py:314
  40.5 0.1 place.1
  40.6 1.9 %collective-permute-start.2 = (f32[64,128]{1,0:T(8,128)S(1)}, f32[64,128]{1,0:T(8,128)S(1)}, u32[]{:S(2)}, u32[]{:S(2)}) collective-permute-start(f32[64,128]{1,0:T(8,128)S(1)} %get-tuple-element.24), channel_id=1, source_target_pairs={{0,1},{1,2},{2,3},{3,4},{4,5},{5,6},{6,7},{7,8},{8,9},{9,10},{10,1... | collective-permute-start | bytes 98312 | tf_op jit(solution)/shard_map/ppermute | solution.py:324
  42.5 4.5 %collective-permute-done.2 = f32[64,128]{1,0:T(8,128)S(1)} collective-permute-done((f32[64,128]{1,0:T(8,128)S(1)}, f32[64,128]{1,0:T(8,128)S(1)}, u32[]{:S(2)}, u32[]{:S(2)}) %collective-permute-start.2) | collective-permute-done | bytes 32800 | tf_op jit(solution)/shard_map/ppermute | solution.py:324
  47.0 0.6 %add.3 = f32[64,128]{1,0:T(8,128)} add(f32[64,128]{1,0:T(8,128)S(1)} %get-tuple-element.23, f32[64,128]{1,0:T(8,128)S(1)} %collective-permute-done.2) | non-fusion elementwise | flops 8192 | bytes 98304 | tf_op jit(solution)/shard_map/add | solution.py:325
Async XLA Ops:
  1.3 14.9 %collective-permute-start = (f32[5,4,512]{2,1,0:T(4,128)S(1)}, f32[5,4,512]{2,1,0:T(4,128)S(1)}, u32[]{:S(2)}, u32[]{:S(2)}) collective-permute-start(f32[5,4,512]{2,1,0:T(4,128)S(1)} %get-tuple-element.18), channel_id=1, source_target_pairs={{0,1},{1,0},{2,3},{3,2},{4,5},{5,4},{6,7},{7,6},{8,9},{9,8},{10,11... | collective-permute-start | bytes 122888 | tf_op jit(solution)/shard_map/ppermute | solution.py:265
  3.3 12.9 %collective-permute-start.1 = (f32[5,4,512]{2,1,0:T(4,128)S(1)}, f32[5,4,512]{2,1,0:T(4,128)S(1)}, u32[]{:S(2)}, u32[]{:S(2)}) collective-permute-start(f32[5,4,512]{2,1,0:T(4,128)S(1)} %get-tuple-element.19), channel_id=1, source_target_pairs={{1,2},{3,4},{5,6},{7,8},{9,10},{11,12},{13,14},{15,16},{17,18},{19... | collective-permute-start | bytes 122888 | tf_op jit(solution)/shard_map/ppermute | solution.py:267
  7.5 14.7 %all-to-all-start = ((f32[16,2,128]{2,1,0:T(2,128)}), f32[16,2,128]{2,1,0:T(2,128)S(1)}, u32[]{:S(2)}, u32[]{:S(2)}) async-start(f32[16,2,128]{2,1,0:T(2,128)} %get-tuple-element.16), calls=%async_computation | async-start | bytes 32768 | tf_op jit(solution)/shard_map/all_to_all | solution.py:264
  40.6 6.4 %collective-permute-start.2 = (f32[64,128]{1,0:T(8,128)S(1)}, f32[64,128]{1,0:T(8,128)S(1)}, u32[]{:S(2)}, u32[]{:S(2)}) collective-permute-start(f32[64,128]{1,0:T(8,128)S(1)} %get-tuple-element.24), channel_id=1, source_target_pairs={{0,1},{1,2},{2,3},{3,4},{4,5},{5,6},{6,7},{7,8},{8,9},{9,10},{10,1... | collective-permute-start | bytes 98312 | tf_op jit(solution)/shard_map/ppermute | solution.py:324

commit v7 on v6

--- a/solution.py
+++ b/solution.py
@@ -54,22 +54,31 @@
     return [mass_flux] + [flow[4] * area[i] + mass_flux * velocity[i] for i in range(3)]
 
 
-def early_kernel(own_ref, offset_ref, flow_ref, area_ref, point_ref, field_ref, spread_ref, own_area_ref, own_point_ref, delay_ref):
+def early_kernel(
+    own_ref, offset_ref, flow_ref, area_ref, point_ref, field_ref, spread_ref, own_area_ref, own_point_ref, delay_ref,
+    held_ref, table_ref, sem,
+):
     width = flow_ref.shape[2]
-    for block in range(delay_ref.shape[0]):
-        delay_ref[block] = offset_ref[own_ref[0], block]
-    own_area_ref[...] = area_ref[...]
-    own_point_ref[...] = point_ref[...]
-    point = [(1.0 / SOUND_STEP) * point_ref[i : i + 1, :] for i in range(3)]
+    routes = ((point_ref, own_point_ref), (area_ref, own_area_ref), (flow_ref, held_ref), (offset_ref, table_ref))
+    copies = [pltpu.make_async_copy(source, target, sem.at[i]) for i, (source, target) in enumerate(routes)]
+    for copy in copies:
+        copy.start()
+    copies[0].wait()
+    point = [(1.0 / SOUND_STEP) * own_point_ref[i : i + 1, :] for i in range(3)]
     reach = RADIUS * RADIUS + point[0] * point[0] + point[1] * point[1] + point[2] * point[2]
     turned = jnp.transpose(jnp.concatenate([2.0 * point[0], 2.0 * point[1], 2.0 * point[2], reach] * 2, axis=0))
+    for i in range(4):
+        spread_ref[i] = jnp.broadcast_to(turned[:, i : i + 1], spread_ref.shape[1:])
+    copies[1].wait()
+    copies[2].wait()
     for cut in range(width // LANES):
         lanes = slice(cut * LANES, (cut + 1) * LANES)
-        area = [area_ref[i : i + 1, lanes] for i in range(3)]
-        for k, field in enumerate(fluxes([flow_ref[i, :, lanes] for i in range(5)], area)):
+        area = [own_area_ref[i : i + 1, lanes] for i in range(3)]
+        for k, field in enumerate(fluxes([held_ref[i, :, lanes] for i in range(5)], area)):
             field_ref[k, cut] = field
-        for i in range(4):
-            spread_ref[i, lanes, :] = jnp.broadcast_to(turned[lanes, i : i + 1], (LANES, LANES))
+    copies[3].wait()
+    for block in range(delay_ref.shape[0]):
+        delay_ref[block] = table_ref[own_ref[0], block]
 
 
 def terms_kernel(time_ref, early_ref, core_ref, chip_ref, area_ref, point_ref, terms_ref, field_ref, part_ref):
@@ -208,8 +217,7 @@
         return carry
 
     lax.fori_loop(0, turns // 2, body, 0)
-    finish(turns - 2, held_ref)
-    rest_ref[...] = multiply(odd_ref, lambda part: None)
+    rest_ref[...] = multiply(odd_ref, lambda part: finish(turns - 2, held_ref) if part == 2 else None)
     finish(turns - 1, rest_ref)
 
 
@@ -277,8 +285,13 @@
             pltpu.VMEM(point_pos.shape, jnp.float32),
             pltpu.SMEM((groups,), jnp.int32),
         ),
-        in_specs=[SMEM] * 2 + [VMEM] * 3,
+        in_specs=[SMEM] + [HBM] * 4,
         out_specs=(VMEM,) * 4 + (SMEM,),
+        scratch_shapes=[
+            pltpu.VMEM(flow.shape, jnp.float32),
+            pltpu.SMEM(band_offset.shape, jnp.int32),
+            pltpu.SemaphoreType.DMA((4,)),
+        ],
         compiler_params=pltpu.CompilerParams(vmem_limit_bytes=16 << 20),
         name="early",
     )(own, in_hbm(band_offset), in_hbm(flow), in_hbm(area_vec), in_hbm(point_pos))

time: 48 us -> 48 us (level)
  no operation moved by 1% of the time
where the time goes in v7:
time: 48 us; the launch traced here: 47.6 us
  starting transfers between devices  15.1 us (31%)
  blocking collectives  11.5 us (24%)
  waiting for transfers between devices  10.3 us (21%)
  Pallas kernels  10.1 us (21%)
  other arithmetic  0.62 us (1%)
    all_to_all x1, blocking collectives, local(): sums = lax.all_to_all(sums, 'obs', 0, 0, tiled=True)  11.5 us
    all_to_all x1, starting transfers between devices, local(): angles = lax.all_to_all(wide, 'obs', 0, 0, tiled=True)  7.05 us
    pallas_call x1, Pallas kernels, local(): pl.pallas_call(pair_kernel, out_shape=pltpu.VMEM((groups, steps, lanes),...  6.8 us
    all_to_all x1, waiting for transfers between devices, local(): angles = lax.all_to_all(wide, 'obs', 0, 0, tiled=True)  5.75 us
    ppermute x1, waiting for transfers between devices, local(): carried = lax.ppermute(later, 'tm', [(i, i + 1) for i in range(times - 1)])  4.52 us
    ppermute x1, starting transfers between devices, local(): from_chip = lax.ppermute(to_chip, 'tm', swaps + [(j, i) for i, j in swaps])  4.23 us
    ppermute x1, starting transfers between devices, local(): from_core = lax.ppermute(to_core, 'tm', [(i, i ^ 1) for i in range(times)])  1.92 us
    ppermute x1, starting transfers between devices, local(): carried = lax.ppermute(later, 'tm', [(i, i + 1) for i in range(times - 1)])  1.92 us
  transfers between devices with their start and end apart: 4, of which 2 were waited for; matrix products, arithmetic and copies ran while one was open for 0% of the time, Pallas kernels for 4%

profile of v7, /device:TPU:384, one launch (start us, length us, event | category | flops | bytes accessed | tf_op | source)
XLA Modules:
  0.0 47.6 jit_solution(6221279289286273892)
XLA Ops:
  0.0 1.3 %prep.1 = (f32[16,2,128]{2,1,0:T(2,128)}, f32[5,4,512]{2,1,0:T(4,128)S(1)}, f32[5,4,512]{2,1,0:T(4,128)S(1)}) custom-call(s32[1]{0:T(128)} %bitcast.1.time_ref, f32[5,64,512]{2,1,0:T(8,128)} %flow_ref.3, f32[2,128]{1,0:T(2,128)} %angle_ref.1), custom_call_target="tpu_custom_call" | custom-call | tf_op jit(solution)/shard_map/prep/pallas_call | solution.py:254
  1.3 1.9 %collective-permute-start = (f32[5,4,512]{2,1,0:T(4,128)S(1)}, f32[5,4,512]{2,1,0:T(4,128)S(1)}, u32[]{:S(2)}, u32[]{:S(2)}) collective-permute-start(f32[5,4,512]{2,1,0:T(4,128)S(1)} %get-tuple-element.18), channel_id=1, source_target_pairs={{0,1},{1,0},{2,3},{3,2},{4,5},{5,4},{6,7},{7,6},{8,9},{9,8},{10,11... | collective-permute-start | bytes 122888 | tf_op jit(solution)/shard_map/ppermute | solution.py:273
  3.3 4.2 %collective-permute-start.1 = (f32[5,4,512]{2,1,0:T(4,128)S(1)}, f32[5,4,512]{2,1,0:T(4,128)S(1)}, u32[]{:S(2)}, u32[]{:S(2)}) collective-permute-start(f32[5,4,512]{2,1,0:T(4,128)S(1)} %get-tuple-element.19), channel_id=1, source_target_pairs={{1,2},{3,4},{5,6},{7,8},{9,10},{11,12},{13,14},{15,16},{17,18},{19... | collective-permute-start | bytes 122888 | tf_op jit(solution)/shard_map/ppermute | solution.py:275
  7.5 7.0 %all-to-all-start = ((f32[16,2,128]{2,1,0:T(2,128)}), f32[16,2,128]{2,1,0:T(2,128)S(1)}, u32[]{:S(2)}, u32[]{:S(2)}) async-start(f32[16,2,128]{2,1,0:T(2,128)} %get-tuple-element.16), calls=%async_computation | async-start | bytes 32768 | tf_op jit(solution)/shard_map/all_to_all | solution.py:272
  14.6 1.3 %early.1 = (f32[4,4,64,128]{3,2,1,0:T(8,128)S(1)}, f32[4,512,128]{2,1,0:T(8,128)S(1)}, f32[3,512]{1,0:T(4,128)S(1)}, f32[3,512]{1,0:T(4,128)S(1)}, s32[16]{0:T(128)S(4)}) custom-call(s32[1]{0:T(128)} %bitcast.own_ref, s32[16,16]{1,0:T(8,128)} %offset_ref.1, f32[5,64,512]{2,1,0:T(8,128)} %flow_ref.3, f32[3,512]{1,0:T(4,128)} %area_ref.1, f32[3,512]{1,0:T(4,128)} %point_ref.1), custom_call_target="tpu_custom_call" | custom-call | tf_op jit(solution)/shard_map/early/pallas_call | solution.py:279
  15.9 0.0 collective-permute-done.core_ref
  15.9 0.0 collective-permute-done.1.chip_ref
  15.9 0.5 terms.1.terms_ref
  16.4 5.8 %all-to-all-done.angle_ref = f32[16,2,128]{2,1,0:T(2,128)S(1)} async-done(((f32[16,2,128]{2,1,0:T(2,128)}), f32[16,2,128]{2,1,0:T(2,128)S(1)}, u32[]{:S(2)}, u32[]{:S(2)}) %all-to-all-start) | async-done | bytes 16416 | tf_op jit(solution)/shard_map/all_to_all | solution.py:272
  22.1 6.8 %pairs.1 = bf16[16,64,128]{2,1,0:T(8,128)(2,1)S(1)} custom-call(f32[16,2,128]{2,1,0:T(2,128)S(1)} %all-to-all-done.angle_ref, bf16[32,256,128]{2,1,0:T(8,128)(2,1)S(1)} %terms.1.terms_ref, f32[4,512,128]{2,1,0:T(8,128)S(1)} %get-tuple-element.22.spread_ref), custom_call_target="tpu_custom_call" | custom-call | tf_op jit(solution)/shard_map/pairs/pallas_call | solution.py:311
  29.0 11.5 %all_to_all.10.sums_ref = bf16[16,64,128]{2,1,0:T(8,128)(2,1)S(1)} all-to-all(bf16[16,64,128]{2,1,0:T(8,128)(2,1)S(1)} %pairs.1), channel_id=1, replica_groups=mesh['obs'=16,'tm'=32] {'obs'}, dimensions={0} | all-to-all | bytes 524288 | tf_op jit(solution)/shard_map/all_to_all | solution.py:327
  40.5 0.1 place.1
  40.6 1.9 %collective-permute-start.2 = (f32[64,128]{1,0:T(8,128)S(1)}, f32[64,128]{1,0:T(8,128)S(1)}, u32[]{:S(2)}, u32[]{:S(2)}) collective-permute-start(f32[64,128]{1,0:T(8,128)S(1)} %get-tuple-element.24), channel_id=1, source_target_pairs={{0,1},{1,2},{2,3},{3,4},{4,5},{5,6},{6,7},{7,8},{8,9},{9,10},{10,1... | collective-permute-start | bytes 98312 | tf_op jit(solution)/shard_map/ppermute | solution.py:337
  42.5 4.5 %collective-permute-done.2 = f32[64,128]{1,0:T(8,128)S(1)} collective-permute-done((f32[64,128]{1,0:T(8,128)S(1)}, f32[64,128]{1,0:T(8,128)S(1)}, u32[]{:S(2)}, u32[]{:S(2)}) %collective-permute-start.2) | collective-permute-done | bytes 32800 | tf_op jit(solution)/shard_map/ppermute | solution.py:337
  47.0 0.6 %add.3 = f32[64,128]{1,0:T(8,128)} add(f32[64,128]{1,0:T(8,128)S(1)} %get-tuple-element.23, f32[64,128]{1,0:T(8,128)S(1)} %collective-permute-done.2) | non-fusion elementwise | flops 8192 | bytes 98304 | tf_op jit(solution)/shard_map/add | solution.py:338
Async XLA Ops:
  1.3 14.6 %collective-permute-start = (f32[5,4,512]{2,1,0:T(4,128)S(1)}, f32[5,4,512]{2,1,0:T(4,128)S(1)}, u32[]{:S(2)}, u32[]{:S(2)}) collective-permute-start(f32[5,4,512]{2,1,0:T(4,128)S(1)} %get-tuple-element.18), channel_id=1, source_target_pairs={{0,1},{1,0},{2,3},{3,2},{4,5},{5,4},{6,7},{7,6},{8,9},{9,8},{10,11... | collective-permute-start | bytes 122888 | tf_op jit(solution)/shard_map/ppermute | solution.py:273
  3.3 12.7 %collective-permute-start.1 = (f32[5,4,512]{2,1,0:T(4,128)S(1)}, f32[5,4,512]{2,1,0:T(4,128)S(1)}, u32[]{:S(2)}, u32[]{:S(2)}) collective-permute-start(f32[5,4,512]{2,1,0:T(4,128)S(1)} %get-tuple-element.19), channel_id=1, source_target_pairs={{1,2},{3,4},{5,6},{7,8},{9,10},{11,12},{13,14},{15,16},{17,18},{19... | collective-permute-start | bytes 122888 | tf_op jit(solution)/shard_map/ppermute | solution.py:275
  7.5 14.7 %all-to-all-start = ((f32[16,2,128]{2,1,0:T(2,128)}), f32[16,2,128]{2,1,0:T(2,128)S(1)}, u32[]{:S(2)}, u32[]{:S(2)}) async-start(f32[16,2,128]{2,1,0:T(2,128)} %get-tuple-element.16), calls=%async_computation | async-start | bytes 32768 | tf_op jit(solution)/shard_map/all_to_all | solution.py:272
  40.6 6.4 %collective-permute-start.2 = (f32[64,128]{1,0:T(8,128)S(1)}, f32[64,128]{1,0:T(8,128)S(1)}, u32[]{:S(2)}, u32[]{:S(2)}) collective-permute-start(f32[64,128]{1,0:T(8,128)S(1)} %get-tuple-element.24), channel_id=1, source_target_pairs={{0,1},{1,2},{2,3},{3,4},{4,5},{5,6},{6,7},{7,8},{8,9},{9,10},{10,1... | collective-permute-start | bytes 98312 | tf_op jit(solution)/shard_map/ppermute | solution.py:337
